TPU v7x, 768 devices: a whole 4x8x12 slice. The times are simulated.
768 devices in a mesh: ct: 16 (over z_hi, y), tile: 48 (over x, z_lo, core).
Axes of the slice: x: 4, y: 8, z: 12 (z_hi: 2, z_lo: 6; z = z_hi * 6 + z_lo), core: 2. Of those that a mesh axis runs over, the one named last changes fastest.
Arguments:
- voltages: int32 [48, 256, 2048], P('tile', 'ct'), may hold values from -8 to 7
- fir_taps: float32 [4, 1024], replicated, may hold values from -3 to 3
- tile_map: int32 [528, 2], P('tile'), may hold values from 0 to 31, as said below
Outputs:
- visibilities: float32 [528, 1024, 128], P('tile', 'ct')
Inputs may be any that keep to these rules, and one draw needn't show every extreme that they name: `tile_map`: each row holds two block numbers, the first not above the second; every such pair of the 32 blocks stands in exactly one row.
All inputs are finite; a program needn't handle non-finite values.
Results may differ from a plain program's by a relative error of at most 0.0056.
Values may be sent and summed in bfloat16 or wider, within the bound.
No kernel may reach another device: no remote copies, remote signals or barrier semaphores. Data moves between devices by JAX's collectives and lax.ppermute only.
A program may use at most 32 MiB of HBM per device.

v0:
```python
import math

import jax
import jax.numpy as jnp
from jax import lax
from jax.sharding import PartitionSpec as P

B = 8


def from_behind(value, axis, steps):
    count = lax.axis_size(axis)
    first, last = (max(0, -steps), min(count, count - steps))
    return lax.ppermute(value, axis, [(source, source + steps) for source in range(first, last)])


def shard_table(channels, shards):
    span = channels // shards
    positions = jnp.arange(channels, dtype=jnp.int32)
    products = positions[:, None] * positions[None, :] % channels
    angles = products.astype(jnp.float32) * (2.0 * math.pi / channels)
    norm_scale = 1.0 / math.sqrt(channels)
    cosine = (jnp.cos(angles) * norm_scale).astype(jnp.bfloat16).reshape(channels, shards, 1, span)
    sine = (jnp.sin(angles) * norm_scale).astype(jnp.bfloat16).reshape(channels, shards, 1, span)
    upper_half = jnp.concatenate([cosine, -sine], axis=2).reshape(channels, 2 * channels)
    lower_half = jnp.concatenate([sine, cosine], axis=2).reshape(channels, 2 * channels)
    return jnp.concatenate([upper_half, lower_half], axis=0)


def tile_sums(arrived, row_blocks, col_blocks, span):
    frame_count = arrived.shape[0]
    block_count = arrived.shape[1] // B
    blocks = arrived.reshape(frame_count, block_count, B, 2, span)
    left_side = jnp.take(blocks, row_blocks, axis=1)
    right_side = jnp.take(blocks, col_blocks, axis=1)
    swapped = jnp.stack([left_side[:, :, :, 1], -left_side[:, :, :, 0]], axis=3)
    stacked = jnp.stack([left_side, swapped], axis=2)
    sums = jnp.einsum(
        "tlqapc,tlbpc->lcqab", stacked, right_side, preferred_element_type=jnp.float32
    )
    return sums.reshape(sums.shape[0], span, 2 * B * B)


def per_device(voltages, fir_taps, tile_map):
    frames, in_dev, row_width = voltages.shape
    channels = row_width // 2
    tap_count = fir_taps.shape[0]
    samples = voltages.astype(jnp.float32) * 0.25
    tap_gains = jnp.concatenate([fir_taps, fir_taps], axis=1)
    extended = jnp.zeros((frames + tap_count - 1, in_dev, row_width), jnp.float32)
    for tap_index in range(tap_count):
        term = tap_gains[tap_index][None, None, :] * samples
        extended = extended + jnp.pad(
            term, ((tap_index, tap_count - 1 - tap_index), (0, 0), (0, 0))
        )
    filtered_sum = extended[:frames]
    spill_over = extended[frames:]
    needed = tap_count - 1
    hop_count = -(-needed // frames)
    for hop_index in range(1, hop_count + 1):
        first_row = (hop_index - 1) * frames
        last_row = min(hop_index * frames, needed)
        incoming = from_behind(spill_over[first_row:last_row], "tile", hop_index)
        filtered_sum = filtered_sum + incoming
    filtered = filtered_sum.astype(jnp.bfloat16)
    shards = lax.axis_size("ct")
    spectra = jnp.dot(
        filtered.reshape(frames * in_dev, row_width),
        shard_table(channels, shards),
        preferred_element_type=jnp.float32,
    ).astype(jnp.bfloat16)
    spectra = spectra.reshape(frames, in_dev, row_width)
    turned = lax.all_to_all(spectra, "ct", split_axis=2, concat_axis=1, tiled=True)
    span = channels // shards
    row_blocks = tile_map[:, 0]
    col_blocks = tile_map[:, 1]
    frame_total = frames * lax.axis_size("tile")
    gathered = lax.all_gather(turned, "tile", axis=0, tiled=True)
    running = tile_sums(gathered, row_blocks, col_blocks, span)
    return running / frame_total


def solution(mesh):
    in_specs = (P("tile", "ct", None), P(), P("tile", None))
    out_specs = P("tile", "ct", None)
    return jax.shard_map(
        per_device, mesh=mesh, in_specs=in_specs, out_specs=out_specs, check_vma=False
    )
```

profile of v0, /device:TPU:1, one launch (start us, length us, event | category | flops | bytes accessed | tf_op | source)
XLA Modules:
  0.0 260.6 jit_solution(5082563366013736770)
XLA Ops:
  6.5 0.0 all-gather.2.cloned.1.call-start
  6.5 0.7 constant_dynamic-update-slice_fusion.1
  7.3 0.7 constant_dynamic-update-slice_fusion
  8.0 0.9 convert_multiply_fusion.3
  9.1 7.2 %collective-permute-start.2 = (f32[1,16,2048]{2,1,0:T(8,128)S(1)}, f32[1,16,2048]{2,1,0:T(8,128)S(1)}, u32[]{:S(2)}, u32[]{:S(2)}) collective-permute-start(f32[1,16,2048]{2,1,0:T(8,128)S(1)} %get-tuple-element.17), channel_id=1, source_target_pairs={{0,3},{1,4},{2,5},{3,6},{4,7},{5,8},{6,9},{7,10},{8,11},{9,12},{10... | collective-permute-start | bytes 393224 | tf_op jit(solution)/shard_map/ppermute | solution.py:14
  16.3 4.0 %collective-permute-start.1 = (f32[1,16,2048]{2,1,0:T(8,128)S(1)}, f32[1,16,2048]{2,1,0:T(8,128)S(1)}, u32[]{:S(2)}, u32[]{:S(2)}) collective-permute-start(f32[1,16,2048]{2,1,0:T(8,128)S(1)} %get-tuple-element.18), channel_id=1, source_target_pairs={{0,2},{1,3},{2,4},{3,5},{4,6},{5,7},{6,8},{7,9},{8,10},{9,11},{10,... | collective-permute-start | bytes 393224 | tf_op jit(solution)/shard_map/ppermute | solution.py:14
  20.3 2.2 collective-permute-start
  22.5 16.9 %fusion.24 = bf16[1024,16,1,64]{0,3,2,1:T(8,128)(2,1)S(1)} fusion(s32[16,64]{1,0:T(8,128)S(1)} %multiply_add_fusion), kind=kLoop, calls=%fused_computation.32 | loop fusion | flops 19922944 | bytes 2101248 | tf_op jit(solution)/shard_map/neg | solution.py:25
  39.4 18.3 %multiply_convert_fusion = (bf16[1024,16,1,64]{0,3,2,1:T(8,128)(2,1)S(1)}, bf16[1024,16,1,64]{0,3,2,1:T(8,128)(2,1)S(1)}) fusion(s32[16,64]{1,0:T(8,128)S(1)} %multiply_add_fusion), kind=kLoop, calls=%fused_computation.19 | loop fusion | flops 18874368 | bytes 4198400 | tf_op jit(solution)/shard_map/convert_element_type | solution.py:24
  57.7 0.6 pad_maximum_fusion
  58.4 0.0 collective-permute-done.2
  58.4 0.0 collective-permute-done.1
  58.4 0.0 collective-permute-done
  58.4 2.3 fusion.19
  60.7 0.0 copy-start.1
  60.7 0.7 copy.27
  61.4 0.5 broadcast.284
  61.9 11.5 %reduce = bf16[2048,16]{1,0:T(8,128)(2,1)S(1)} reduce(bf16[2048,1,16]{2,1,0:T(2,128)(2,1)S(1)} %bitcast.48, bf16[]{:T(256)} %broadcast.284), dimensions={1}, to_apply=%bitcast.40.reduce_sub_computation | reduce | bytes 131074
  73.5 0.6 reshape.195
  74.0 31.1 %all_to_all.18 = bf16[16,2,1024]{2,1,0:T(2,128)(2,1)S(1)} all-to-all(bf16[16,2,1024]{2,1,0:T(2,128)(2,1)S(1)} %reshape.195), channel_id=1, replica_groups=mesh['ct'=16,'tile'=48] {'ct'}, dimensions={0} | all-to-all | bytes 131072 | tf_op jit(solution)/shard_map/all_to_all | solution.py:73
  105.1 0.9 reshape.196
  106.0 0.5 copy.28
  106.6 0.6 copy.29
  107.2 0.0 all-gather.2.cloned.1.call-update
  107.2 0.0 copy-done.1
  107.3 92.6 %all-gather.2.cloned.1.call-done = bf16[48,256,128]{2,1,0:T(8,128)(2,1)} async-done(((bf16[1,256,128]{2,1,0:T(8,128)(2,1)}), bf16[48,256,128]{2,1,0:T(8,128)(2,1)}) %all-gather.2.cloned.1.call-update) | async-done | bytes 3145744 | tf_op jit(solution)/shard_map/all_gather | solution.py:78
  199.9 11.6 %reshape.170 = bf16[48,32,8,2,64]{4,3,2,1,0:T(2,128)(2,1)} reshape(bf16[48,256,128]{2,1,0:T(8,128)(2,1)} %all-gather.2.cloned.1.call-done) | data formatting | bytes 6291456 | tf_op jit(solution)/shard_map/reshape | solution.py:33
  211.5 7.1 %copy.30 = bf16[48,32,8,2,64]{4,2,3,1,0:T(8,128)(2,1)} copy(bf16[48,32,8,2,64]{4,3,2,1,0:T(2,128)(2,1)} %reshape.170) | data formatting | bytes 6291456 | tf_op jit(solution)/shard_map/reshape | solution.py:33
  218.6 5.2 %gather_fusion.1 = bf16[11,48,8,2,64]{4,2,3,1,0:T(8,128)(2,1)} fusion(bf16[48,32,8,2,64]{4,2,3,1,0:T(8,128)(2,1)} %copy.30, s32[1024]{0:T(1024)S(1)} %get-tuple-element.31), kind=kCustom, calls=%fused_computation.1.clone | custom fusion | bytes 2162732 | tf_op jit(solution)/shard_map/jit(_take)/gather | solution.py:35
  223.8 1.9 select_bitcast_fusion
  225.7 5.5 %copy.37 = bf16[48,11,8,2,64,1]{0,2,3,5,4,1:T(8,128)(2,1)} copy(bf16[48,11,8,2,64,1]{4,2,3,0,1,5:T(8,128)(2,1)S(1)} %select_bitcast_fusion) | data formatting | bytes 2162688 | tf_op jit(solution)/shard_map/jit(_take)/select_n | solution.py:35
  231.2 5.2 %gather_fusion = bf16[11,48,8,2,64]{4,2,3,1,0:T(8,128)(2,1)} fusion(bf16[48,32,8,2,64]{4,2,3,1,0:T(8,128)(2,1)} %copy.30, s32[1024]{0:T(1024)S(1)} %get-tuple-element.32), kind=kCustom, calls=%fused_computation.clone | custom fusion | bytes 2162732 | tf_op jit(solution)/shard_map/jit(_take)/gather | solution.py:34
  236.4 5.3 %copy.31 = bf16[11,48,8,2,64]{1,2,3,4,0:T(8,128)(2,1)S(1)} copy(bf16[11,48,8,2,64]{4,2,3,1,0:T(8,128)(2,1)} %gather_fusion) | data formatting | bytes 2162688 | tf_op jit(solution)/shard_map/jit(_take)/gather | solution.py:34
  241.7 0.4 fusion.22
  242.1 0.4 fusion.32
  242.5 0.0 copy-start
  242.5 0.7 maximum_bitcast_fusion
  243.2 1.1 copy-done
  244.3 3.7 %bitcast_multiply_fusion = f32[11,64,2,8,8]{4,3,2,1,0:T(8,128)} fusion(bf16[48,11,8,2,64,1]{0,2,3,5,4,1:T(8,128)(2,1)S(1)} %copy-done, bf16[48,11,1,8,2,64]{0,3,4,2,5,1:T(8,128)(2,1)S(1)} %maximum_bitcast_fusion, bf16[48,11,1,8,2,64]{0,3,4,2,5,1:T(8,128)(2,1)S(1)} %get-tuple-element.10), kind=kOutput, calls=%fused_computation.13 | convolution fusion | flops 18472960 | bytes 3604480 | tf_op jit(solution)/shard_map/tlqapc,tlbpc->lcqab/dot_general | solution.py:38
  248.1 4.7 %copy.35 = f32[11,64,2,8,8]{1,4,3,2,0:T(8,128)S(1)} copy(f32[11,64,2,8,8]{4,3,2,1,0:T(8,128)} %bitcast_multiply_fusion) | data formatting | bytes 720896 | tf_op jit(solution)/shard_map/div | solution.py:80
  252.8 1.0 copy.36
  (8 shorter events, 0.1 us)
Async XLA Ops:
  6.5 193.4 %all-gather.2.cloned.1.call-start = ((), (), s32[]{:S(2)}) async-start(), calls=%async_computation.1 | async-start | bytes 3211264 | tf_op jit(solution)/shard_map/all_gather | solution.py:78
  9.1 49.3 %collective-permute-start.2 = (f32[1,16,2048]{2,1,0:T(8,128)S(1)}, f32[1,16,2048]{2,1,0:T(8,128)S(1)}, u32[]{:S(2)}, u32[]{:S(2)}) collective-permute-start(f32[1,16,2048]{2,1,0:T(8,128)S(1)} %get-tuple-element.17), channel_id=1, source_target_pairs={{0,3},{1,4},{2,5},{3,6},{4,7},{5,8},{6,9},{7,10},{8,11},{9,12},{10... | collective-permute-start | bytes 393224 | tf_op jit(solution)/shard_map/ppermute | solution.py:14
  16.3 42.1 %collective-permute-start.1 = (f32[1,16,2048]{2,1,0:T(8,128)S(1)}, f32[1,16,2048]{2,1,0:T(8,128)S(1)}, u32[]{:S(2)}, u32[]{:S(2)}) collective-permute-start(f32[1,16,2048]{2,1,0:T(8,128)S(1)} %get-tuple-element.18), channel_id=1, source_target_pairs={{0,2},{1,3},{2,4},{3,5},{4,6},{5,7},{6,8},{7,9},{8,10},{9,11},{10,... | collective-permute-start | bytes 393224 | tf_op jit(solution)/shard_map/ppermute | solution.py:14
  20.3 38.1 %collective-permute-start = (f32[1,16,2048]{2,1,0:T(8,128)S(1)}, f32[1,16,2048]{2,1,0:T(8,128)S(1)}, u32[]{:S(2)}, u32[]{:S(2)}) collective-permute-start(f32[1,16,2048]{2,1,0:T(8,128)S(1)} %get-tuple-element.16), channel_id=1, source_target_pairs={{0,1},{1,2},{2,3},{3,4},{4,5},{5,6},{6,7},{7,8},{8,9},{9,10},{10,1... | collective-permute-start | bytes 393224 | tf_op jit(solution)/shard_map/ppermute | solution.py:14
  60.7 46.6 %copy-start.1 = (s32[11,2]{0,1:T(2,128)S(1)}, s32[11,2]{0,1:T(2,128)}, u32[]{:S(2)}) copy-start(s32[11,2]{0,1:T(2,128)} %param.7) | copy-start | bytes 268
  242.5 1.8 copy-start
Sparse Core Ops, SparseCore 0:
  107.4 92.5 all-gather.1
where the time goes:
time: 261 us
  waiting for transfers between devices  92.6 us (35%)
  local copies, waits for them, and re-layouts  52.1 us (20%)
  other arithmetic  51.8 us (20%)
  blocking collectives  31.1 us (12%)
  between operations  13.6 us (5%)
  starting transfers between devices  13.4 us (5%)
  matrix products  5.99 us (2%)
    all_gather x1, waiting for transfers between devices, per_device(): gathered = lax.all_gather(turned, 'tile', axis=0, tiled=True)  92.6 us
    all_to_all x1, blocking collectives, per_device(): lax.all_to_all(spectra, 'ct', split_axis=2, concat_axis=1, tiled=True)  31.1 us
    reshape x2, local copies, waits for them, and re-layouts, tile_sums(): blocks = arrived.reshape(frame_count, block_count, B, 2, span)  18.7 us
    convert_element_type x1, other arithmetic, shard_table(): (jnp.sin(angles) * norm_scale).astype(jnp.bfloat16)  18.3 us
    neg x1, other arithmetic, shard_table(): -sine  16.9 us
    ppermute x3, starting transfers between devices, from_behind(): lax.ppermute(value, axis, [(source, source + steps) for source in range(f...  13.4 us
    unnamed x1, other arithmetic  11.5 us
    gather x2, local copies, waits for them, and re-layouts, tile_sums(): left_side = jnp.take(blocks, row_blocks, axis=1)  10.5 us
  transfers between devices with their start and end apart: 4, of which 1 were waited for; matrix products, arithmetic and copies ran while one was open for 14% of the time, Pallas kernels for 0%

commit v1 on v0

v1 whole, which is shorter than its diff:
```python
import math

import jax
import jax.numpy as jnp
import ml_dtypes
import numpy as np
from jax import lax
from jax.experimental import pallas as pl
from jax.experimental.pallas import tpu as pltpu
from jax.sharding import Mesh, PartitionSpec as P

NCHAN = 1024
TIME = 48
LANES = 128
ZH, Y, X, ZQ, ZR, C = 2, 8, 4, 3, 2, 2
TILE_AXES = ("x", "zq", "zr", "c")
OWN = 11
VMEM = 48 * 1024 * 1024

BF = jnp.bfloat16
F32 = jnp.float32


def dft_tables():
    y, x, zh, zr, c = np.meshgrid(*(np.arange(n) for n in (Y, X, ZH, ZR, C)), indexing="ij")
    first = ((zh * Y + y) * 64 + ((x * ZR + zr) * C + c) * 4).reshape(-1)
    channels = first[None, :] + np.arange(4)[:, None]
    products = channels[:, :, None] * np.arange(NCHAN)[None, None, :] % NCHAN
    angles = products.astype(np.float32) * np.float32(2.0 * math.pi / NCHAN)
    scale = np.float32(1.0 / math.sqrt(NCHAN))
    return tuple((f(angles) * scale).astype(ml_dtypes.bfloat16) for f in (np.cos, np.sin))


def swap_chunks(rows, width):
    rows = list(rows)
    chunk = lax.broadcasted_iota(jnp.int32, rows[0].shape, 1) // width
    step = len(rows) // 2
    while step:
        low = (chunk & step) == 0
        for g in range(len(rows)):
            if not g & step:
                a, b = rows[g], rows[g + step]
                rows[g] = jnp.where(low, a, pltpu.roll(b, step * width, 1))
                rows[g + step] = jnp.where(low, pltpu.roll(a, LANES - step * width, 1), b)
        step //= 2
    return rows


def dot(a, b, contract):
    return lax.dot_general(a, b, ((contract[:1], contract[1:]), ((), ())), preferred_element_type=F32)


def filter_kernel(map_ref, v0_ref, v1_ref, v2_ref, v3_ref, fir_ref, cos_ref, sin_ref, out_ref, w_ref, acc_ref):
    step = pl.program_id(0)

    @pl.when(step == 0)
    def _():
        halves = []
        for p in range(2):
            total = None
            for k, ref in enumerate((v0_ref, v1_ref, v2_ref, v3_ref)):
                part = ref[:, p * NCHAN : (p + 1) * NCHAN].astype(F32) * 0.25
                term = fir_ref[k : k + 1, :] * part
                total = term if total is None else total + term
            halves.append(total.astype(BF).astype(F32))
        re, im = halves
        w_ref[0] = jnp.concatenate([re, im] * 4, axis=0).astype(BF)
        w_ref[1] = jnp.concatenate([im, -re] * 4, axis=0).astype(BF)
        acc_ref[...] = jnp.zeros_like(acc_ref)

    block = lax.broadcasted_iota(jnp.int32, (LANES, NCHAN), 0) // 32
    here = block == step
    total = acc_ref[...]
    for i, ref in enumerate((cos_ref, sin_ref)):
        weights = jnp.where(here, w_ref[i].astype(F32), 0.0).astype(BF)
        total = total + dot(ref[0], weights, (1, 1))
    acc_ref[...] = total

    @pl.when(step == pl.num_programs(0) - 1)
    def _():
        own = (lax.axis_index("x") * ZR + lax.axis_index("zr")) * C + lax.axis_index("c")
        sub = lax.broadcasted_iota(jnp.int32, (8, LANES), 0)
        place = lax.broadcasted_iota(jnp.int32, (8, LANES), 1) + (sub % 2) * LANES - own * 16
        tiles = jnp.zeros((8, LANES), jnp.int32)
        for l in range(OWN):
            tiles = jnp.where(place == l, jnp.where(sub < 2, map_ref[0, l], map_ref[1, l]), tiles)
        tiles = jnp.where(sub < 4, tiles, 0).astype(F32)
        data = acc_ref[...].reshape(Y * X, 8, LANES)
        both = jnp.concatenate([data, jnp.broadcast_to(tiles[None], data.shape)], axis=1)
        out_ref[...] = both.astype(BF)


def turn_kernel(in_ref, out_ref, f_ref):
    f_ref[...] = in_ref[...].astype(F32).reshape(f_ref.shape)
    tiles = sum(f_ref[x * 16 + 8 : x * 16 + 16, :] for x in range(X))
    for zh in range(ZH):
        for z in range(ZR * C):
            d = zh * ZR * C + z
            rows = [f_ref[pl.ds(x * 16 + d, Y, stride=64), :] for x in range(X)]
            block = jnp.concatenate(rows + [tiles], axis=0).astype(BF)
            for zq in range(ZQ):
                out_ref[(zh * ZQ + zq) * ZR * C + z] = block


def correlate_kernel(in_ref, out_ref, f_ref, a_ref, c_ref, d_ref):
    f_ref[: 24 * 40] = in_ref[...].astype(F32).reshape(24 * 40, LANES)
    f_ref[24 * 40 :] = jnp.zeros((64, LANES), F32)
    row = lax.broadcasted_iota(jnp.int32, (64, LANES), 0)
    frame = (row % 5 != 4) & (row < 60)
    for zh in range(ZH):
        groups = [jnp.where(frame, f_ref[pl.ds(zh * 480 + y, 64, stride=8), :], 0.0) for y in range(Y)]
        for k, part in enumerate(swap_chunks(groups, 16)):
            ch, p = divmod(k, 2)
            a_ref[ch, p * 64 : (p + 1) * 64, zh * LANES : (zh + 1) * LANES] = part.astype(BF)

    i = lax.broadcasted_iota(jnp.int32, (256, 256), 0)
    j = lax.broadcasted_iota(jnp.int32, (256, 256), 1)
    order = jnp.where(i == (j % 32) * 8 + j // 32, 1.0, 0.0).astype(BF)
    for ch in range(4):
        cols = a_ref[ch]
        left = dot(cols, order, (1, 0))
        re, im = left[:64], left[64:]
        both = jnp.concatenate([jnp.concatenate([re, im], axis=0), jnp.concatenate([im, -re], axis=0)], axis=1)
        c_ref[...] = dot(both.astype(BF), cols, (0, 0)) * (1.0 / TIME)
        for block, (h, g) in enumerate(((0, 0), (1, 0), (1, 1))):
            rows = [c_ref[k * 32 + g * 16 : k * 32 + g * 16 + 16, h * LANES : (h + 1) * LANES] for k in range(16)]
            for s, part in enumerate(swap_chunks(rows, 8)):
                at = block * 256 + s * 16
                d_ref[at : at + 16, ch * LANES : (ch + 1) * LANES] = part.astype(BF)

    first = lax.axis_index("zq") * 160 + 32
    tiles = sum(f_ref[pl.ds(pl.multiple_of(first + 40 * k, 8), 8), :] for k in range(ZR * C))
    r = jnp.concatenate([tiles[0:1], tiles[1:2]], axis=1).astype(jnp.int32)
    s = jnp.concatenate([tiles[2:3], tiles[3:4]], axis=1).astype(jnp.int32)
    rh, sh = jnp.where(r >= 16, 1, 0), jnp.where(s >= 16, 1, 0)
    index = (rh + sh) * 256 + (s - 16 * sh) * 16 + (r - 16 * rh)
    pick = jnp.where(lax.broadcasted_iota(jnp.int32, (768, 256), 0) == index, 1.0, 0.0).astype(BF)
    picked = dot(pick, d_ref[...], (0, 0)).astype(BF)
    for d in range(16):
        for ch in range(4):
            out_ref[d, ch * 16 : (ch + 1) * 16, :] = picked[d * 16 : (d + 1) * 16, ch * LANES : (ch + 1) * LANES]


def place_kernel(in_ref, out_ref, f_ref):
    f_ref[...] = in_ref[...].astype(F32).reshape(f_ref.shape)
    for l in range(OWN):
        out_ref[l] = f_ref[pl.ds(l, 64, stride=16), :]


PARAMS = pltpu.CompilerParams(vmem_limit_bytes=VMEM)


def per_device(voltages, fir_taps, tile_map):
    own = voltages[0].astype(BF)
    count = X * ZQ * ZR * C
    before = [lax.ppermute(own, TILE_AXES, [(t, t + k) for t in range(count - k)]) for k in (1, 2, 3)]
    cos, sin = dft_tables()
    whole = lambda *shape: pl.BlockSpec(shape, lambda j: (0,) * len(shape))
    table = pl.BlockSpec((1, 256, NCHAN), lambda j: (j, 0, 0))
    sent = pl.pallas_call(
        filter_kernel,
        out_shape=jax.ShapeDtypeStruct((Y * X, 16, LANES), BF),
        grid=(4,),
        in_specs=[pl.BlockSpec(memory_space=pltpu.SMEM)]
        + [whole(16, 2 * NCHAN)] * 4
        + [whole(4, NCHAN), table, table],
        out_specs=whole(Y * X, 16, LANES),
        scratch_shapes=[pltpu.VMEM((2, LANES, NCHAN), BF), pltpu.VMEM((256, LANES), F32)],
        compiler_params=PARAMS,
        name="filter",
    )(tile_map.T, own, *before, fir_taps, jnp.asarray(cos), jnp.asarray(sin))
    came = lax.all_to_all(sent, ("y", "x"), 0, 0, tiled=True)
    sent = pl.pallas_call(
        turn_kernel,
        out_shape=jax.ShapeDtypeStruct((ZH * ZQ * ZR * C, 40, LANES), BF),
        scratch_shapes=[pltpu.VMEM((Y * X * 16, LANES), F32)],
        compiler_params=PARAMS,
        name="turn",
    )(came)
    came = lax.all_to_all(sent, ("zh", "zq", "zr", "c"), 0, 0, tiled=True)
    sent = pl.pallas_call(
        correlate_kernel,
        out_shape=jax.ShapeDtypeStruct((16, 64, LANES), BF),
        scratch_shapes=[
            pltpu.VMEM((1024, LANES), F32),
            pltpu.VMEM((4, LANES, 256), BF),
            pltpu.VMEM((512, 256), F32),
            pltpu.VMEM((768, 512), BF),
        ],
        compiler_params=PARAMS,
        name="correlate",
    )(came)
    came = lax.all_to_all(sent, ("x", "zr", "c"), 0, 0, tiled=True)
    return pl.pallas_call(
        place_kernel,
        out_shape=jax.ShapeDtypeStruct((OWN, 64, LANES), F32),
        scratch_shapes=[pltpu.VMEM((1024, LANES), F32)],
        compiler_params=PARAMS,
        name="place",
    )(came)


def solution(mesh):
    fine = Mesh(mesh.devices.reshape(ZH, Y, X, ZQ, ZR, C), ("zh", "y") + TILE_AXES)
    in_specs = (P(TILE_AXES, ("zh", "y"), None), P(), P(TILE_AXES, None))
    out_specs = P(TILE_AXES, ("zh", "y"), None)
    return jax.shard_map(per_device, mesh=fine, in_specs=in_specs, out_specs=out_specs, check_vma=False)
```

time: 261 us -> 92.1 us (0.35)
  waiting for transfers between devices: 92.6 us -> 1.84 us
  other arithmetic: 51.8 us -> 0.91 us
  local copies, waits for them, and re-layouts: 52.1 us -> 4.58 us
  blocking collectives: 31.1 us -> 64.9 us
  between operations: 13.6 us -> 0.07 us
  matrix products: 5.99 us -> 0 us
  Pallas kernels: 0 us -> 5.97 us
    all_gather x1 -> x0, waiting for transfers between devices: 92.6 us -> none  [per_device(): gathered = lax.all_gather(turned, 'tile', axis=0, tiled=True)]
    all_to_all x1 -> x3, blocking collectives: 31.1 us -> 64.9 us  [the longest x1 31.7 us: per_device(): came = lax.all_to_all(sent, ('zh', 'zq', 'zr', 'c'), 0, 0, tiled=True)]
    reshape x3 -> x0, local copies, waits for them, and re-layouts: 19.4 us -> none  [the longest x2 18.7 us: tile_sums(): blocks = arrived.reshape(frame_count, block_count, B, 2, span)]
    convert_element_type x1, other arithmetic: 18.3 us -> 0.91 us  [per_device(): own = voltages[0].astype(BF)]
    neg x1 -> x0, other arithmetic: 16.9 us -> none  [shard_table(): -sine]
    gather x3 -> x0, local copies, waits for them, and re-layouts: 15.7 us -> none  [the longest x2 10.5 us: tile_sums(): left_side = jnp.take(blocks, row_blocks, axis=1)]
    unnamed x1 -> x0, other arithmetic: 11.5 us -> none
    dot_general x2 -> x0, matrix products: 5.99 us -> none  [the longest x1 3.73 us: tile_sums(): jnp.einsum('tlqapc,tlbpc->lcqab', stacked, right_side, preferred_element_...]
  transfers between devices with their start and end apart: 4 -> 3, of which waited for: 1 -> 1; matrix products, arithmetic and copies ran while one was open for 14% -> 0% of each run, Pallas kernels for 0% -> 0%
where the time goes in v1:
time: 92.1 us; the launch traced here: 91.7 us
  blocking collectives  64.9 us (70%)
  starting transfers between devices  13.4 us (15%)
  Pallas kernels  5.97 us (6%)
  local copies, waits for them, and re-layouts  4.58 us (5%)
  waiting for transfers between devices  1.84 us (2%)
    all_to_all x1, blocking collectives, per_device(): came = lax.all_to_all(sent, ('zh', 'zq', 'zr', 'c'), 0, 0, tiled=True)  31.7 us
    all_to_all x1, blocking collectives, per_device(): came = lax.all_to_all(sent, ('y', 'x'), 0, 0, tiled=True)  22.2 us
    ppermute x3, starting transfers between devices, per_device(): lax.ppermute(own, TILE_AXES, [(t, t + k) for t in range(count - k)])  13.4 us
    all_to_all x1, blocking collectives, per_device(): came = lax.all_to_all(sent, ('x', 'zr', 'c'), 0, 0, tiled=True)  11.1 us
    unnamed x8, local copies, waits for them, and re-layouts  4.58 us
    pallas_call x1, Pallas kernels, per_device(): pl.pallas_call(filter_kernel, out_shape=jax.ShapeDtypeStruct((Y * X, 16,...  2.58 us
    pallas_call x1, Pallas kernels, per_device(): pl.pallas_call(correlate_kernel, out_shape=jax.ShapeDtypeStruct((16, 64,...  2.41 us
  transfers between devices with their start and end apart: 3, of which 1 were waited for; matrix products, arithmetic and copies ran while one was open for 0% of the time, Pallas kernels for 0%

profile of v1, /device:TPU:1, one launch (start us, length us, event | category | flops | bytes accessed | tf_op | source)
XLA Modules:
  0.0 91.7 jit_solution(653447901527755599)
XLA Ops:
  0.0 0.9 convert_bitcast_fusion.v0_ref
  0.9 7.2 %collective-permute-start.2 = (bf16[16,2048]{1,0:T(8,128)(2,1)S(1)}, bf16[16,2048]{1,0:T(8,128)(2,1)S(1)}, u32[]{:S(2)}, u32[]{:S(2)}) collective-permute-start(bf16[16,2048]{1,0:T(8,128)(2,1)S(1)} %convert_bitcast_fusion.v0_ref), channel_id=1, source_target_pairs={{0,3},{1,4},{2,5},{3,6},{4,7},{5,8},{6,9},{7,10},{8,11},{9,12},{10... | collective-permute-start | bytes 196616 | tf_op jit(solution)/shard_map/ppermute | solution.py:156
  8.1 4.0 %collective-permute-start.1 = (bf16[16,2048]{1,0:T(8,128)(2,1)S(1)}, bf16[16,2048]{1,0:T(8,128)(2,1)S(1)}, u32[]{:S(2)}, u32[]{:S(2)}) collective-permute-start(bf16[16,2048]{1,0:T(8,128)(2,1)S(1)} %convert_bitcast_fusion.v0_ref), channel_id=1, source_target_pairs={{0,2},{1,3},{2,4},{3,5},{4,6},{5,7},{6,8},{7,9},{8,10},{9,11},{10,... | collective-permute-start | bytes 196616 | tf_op jit(solution)/shard_map/ppermute | solution.py:156
  12.1 2.2 %collective-permute-start = (bf16[16,2048]{1,0:T(8,128)(2,1)S(1)}, bf16[16,2048]{1,0:T(8,128)(2,1)S(1)}, u32[]{:S(2)}, u32[]{:S(2)}) collective-permute-start(bf16[16,2048]{1,0:T(8,128)(2,1)S(1)} %convert_bitcast_fusion.v0_ref), channel_id=1, source_target_pairs={{0,1},{1,2},{2,3},{3,4},{4,5},{5,6},{6,7},{7,8},{8,9},{9,10},{10,1... | collective-permute-start | bytes 196616 | tf_op jit(solution)/shard_map/ppermute | solution.py:156
  14.3 0.0 collective-permute-done.2.v3_ref
  14.3 0.0 collective-permute-done.1.v2_ref
  14.4 1.8 %collective-permute-done.v1_ref = bf16[16,2048]{1,0:T(8,128)(2,1)S(1)} collective-permute-done((bf16[16,2048]{1,0:T(8,128)(2,1)S(1)}, bf16[16,2048]{1,0:T(8,128)(2,1)S(1)}, u32[]{:S(2)}, u32[]{:S(2)}) %collective-permute-start) | collective-permute-done | bytes 65568 | tf_op jit(solution)/shard_map/ppermute | solution.py:156
  16.2 0.0 copy-start
  16.2 1.6 %copy-done = bf16[4,256,1024]{2,1,0:T(8,128)(2,1)S(1)} copy-done((bf16[4,256,1024]{2,1,0:T(8,128)(2,1)S(1)}, bf16[4,256,1024]{2,1,0:T(8,128)(2,1)}, u32[]{:S(2)}) %copy-start) | copy-done | bytes 2097176
  17.8 0.0 copy-start.1
  17.8 1.6 %copy-done.1 = bf16[4,256,1024]{2,1,0:T(8,128)(2,1)S(1)} copy-done((bf16[4,256,1024]{2,1,0:T(8,128)(2,1)S(1)}, bf16[4,256,1024]{2,1,0:T(8,128)(2,1)}, u32[]{:S(2)}) %copy-start.1) | copy-done | bytes 2097176
  19.4 0.0 copy-start.2
  19.4 0.7 copy-done.2
  20.1 0.0 copy-start.3
  20.1 0.7 copy-done.3
  20.8 2.6 %filter.1 = bf16[32,16,128]{2,1,0:T(8,128)(2,1)S(1)} custom-call(s32[2,11]{1,0:T(2,128)S(1)} %bitcast.3, bf16[16,2048]{1,0:T(8,128)(2,1)S(1)} %convert_bitcast_fusion.v0_ref, bf16[16,2048]{1,0:T(8,128)(2,1)S(1)} %collective-permute-done.v1_ref, bf16[16,2048]{1,0:T(8,128)(2,1)S(1)} %collective-permute-done.1.v2_ref, ...), custom_call_target="tpu_custom_call" | custom-call | tf_op jit(solution)/shard_map/filter/pallas_call | solution.py:160
  23.4 22.2 %all_to_all.15.in_ref = bf16[32,16,128]{2,1,0:T(8,128)(2,1)S(1)} all-to-all(bf16[32,16,128]{2,1,0:T(8,128)(2,1)S(1)} %filter.1), channel_id=1, replica_groups=mesh['zh'=2,'y'=8,'x'=4,'zq'=3,'zr'=2,'c'=2] {'y','x'}, dimensions={0} | all-to-all | bytes 262144 | tf_op jit(solution)/shard_map/all_to_all | solution.py:172
  45.5 0.1 turn.1
  45.6 31.7 %all_to_all.16.in_ref = bf16[24,40,128]{2,1,0:T(8,128)(2,1)S(1)} all-to-all(bf16[24,40,128]{2,1,0:T(8,128)(2,1)S(1)} %turn.1), channel_id=1, replica_groups=mesh['zh'=2,'y'=8,'x'=4,'zq'=3,'zr'=2,'c'=2] {'zh','zq','zr','c'}, dimensions={0} | all-to-all | bytes 491520 | tf_op jit(solution)/shard_map/all_to_all | solution.py:180
  77.3 2.4 %correlate.1 = bf16[16,64,128]{2,1,0:T(8,128)(2,1)S(1)} custom-call(bf16[24,40,128]{2,1,0:T(8,128)(2,1)S(1)} %all_to_all.16.in_ref), custom_call_target="tpu_custom_call" | custom-call | tf_op jit(solution)/shard_map/correlate/pallas_call | solution.py:181
  79.7 11.1 %all_to_all.17.in_ref = bf16[16,64,128]{2,1,0:T(8,128)(2,1)S(1)} all-to-all(bf16[16,64,128]{2,1,0:T(8,128)(2,1)S(1)} %correlate.1), channel_id=1, replica_groups=mesh['zh'=2,'y'=8,'x'=4,'zq'=3,'zr'=2,'c'=2] {'x','zr','c'}, dimensions={0} | all-to-all | bytes 524288 | tf_op jit(solution)/shard_map/all_to_all | solution.py:193
  90.8 0.9 place.1
Async XLA Ops:
  0.9 13.4 %collective-permute-start.2 = (bf16[16,2048]{1,0:T(8,128)(2,1)S(1)}, bf16[16,2048]{1,0:T(8,128)(2,1)S(1)}, u32[]{:S(2)}, u32[]{:S(2)}) collective-permute-start(bf16[16,2048]{1,0:T(8,128)(2,1)S(1)} %convert_bitcast_fusion.v0_ref), channel_id=1, source_target_pairs={{0,3},{1,4},{2,5},{3,6},{4,7},{5,8},{6,9},{7,10},{8,11},{9,12},{10... | collective-permute-start | bytes 196616 | tf_op jit(solution)/shard_map/ppermute | solution.py:156
  8.1 6.2 %collective-permute-start.1 = (bf16[16,2048]{1,0:T(8,128)(2,1)S(1)}, bf16[16,2048]{1,0:T(8,128)(2,1)S(1)}, u32[]{:S(2)}, u32[]{:S(2)}) collective-permute-start(bf16[16,2048]{1,0:T(8,128)(2,1)S(1)} %convert_bitcast_fusion.v0_ref), channel_id=1, source_target_pairs={{0,2},{1,3},{2,4},{3,5},{4,6},{5,7},{6,8},{7,9},{8,10},{9,11},{10,... | collective-permute-start | bytes 196616 | tf_op jit(solution)/shard_map/ppermute | solution.py:156
  12.1 4.1 %collective-permute-start = (bf16[16,2048]{1,0:T(8,128)(2,1)S(1)}, bf16[16,2048]{1,0:T(8,128)(2,1)S(1)}, u32[]{:S(2)}, u32[]{:S(2)}) collective-permute-start(bf16[16,2048]{1,0:T(8,128)(2,1)S(1)} %convert_bitcast_fusion.v0_ref), channel_id=1, source_target_pairs={{0,1},{1,2},{2,3},{3,4},{4,5},{5,6},{6,7},{7,8},{8,9},{9,10},{10,1... | collective-permute-start | bytes 196616 | tf_op jit(solution)/shard_map/ppermute | solution.py:156
  16.2 1.6 %copy-start = (bf16[4,256,1024]{2,1,0:T(8,128)(2,1)S(1)}, bf16[4,256,1024]{2,1,0:T(8,128)(2,1)}, u32[]{:S(2)}) copy-start(bf16[4,256,1024]{2,1,0:T(8,128)(2,1)} %constant.5.clone.sin_ref) | copy-start | bytes 6291460
  17.8 1.6 %copy-start.1 = (bf16[4,256,1024]{2,1,0:T(8,128)(2,1)S(1)}, bf16[4,256,1024]{2,1,0:T(8,128)(2,1)}, u32[]{:S(2)}) copy-start(bf16[4,256,1024]{2,1,0:T(8,128)(2,1)} %constant.4.clone.cos_ref) | copy-start | bytes 6291460
  19.4 0.7 copy-start.2
  20.1 0.7 copy-start.3

commit v2 on v1

--- a/solution.py
+++ b/solution.py
@@ -10,25 +10,28 @@
 from jax.sharding import Mesh, PartitionSpec as P
 
 NCHAN = 1024
+QUARTER = NCHAN // 4
 TIME = 48
 LANES = 128
 ZH, Y, X, ZQ, ZR, C = 2, 8, 4, 3, 2, 2
 TILE_AXES = ("x", "zq", "zr", "c")
 OWN = 11
+SLOT = 12
 VMEM = 48 * 1024 * 1024
 
 BF = jnp.bfloat16
 F32 = jnp.float32
 
 
-def dft_tables():
+def dft_table():
     y, x, zh, zr, c = np.meshgrid(*(np.arange(n) for n in (Y, X, ZH, ZR, C)), indexing="ij")
     first = ((zh * Y + y) * 64 + ((x * ZR + zr) * C + c) * 4).reshape(-1)
-    channels = first[None, :] + np.arange(4)[:, None]
-    products = channels[:, :, None] * np.arange(NCHAN)[None, None, :] % NCHAN
+    channels = first[:, None] + np.arange(4)[None, :]
+    products = channels[:, :, None] * np.arange(QUARTER)[None, None, :] % NCHAN
     angles = products.astype(np.float32) * np.float32(2.0 * math.pi / NCHAN)
     scale = np.float32(1.0 / math.sqrt(NCHAN))
-    return tuple((f(angles) * scale).astype(ml_dtypes.bfloat16) for f in (np.cos, np.sin))
+    both = np.stack([np.cos(angles) * scale, np.sin(angles) * scale], axis=2)
+    return both.reshape(256, 8 * QUARTER).astype(ml_dtypes.bfloat16)
 
 
 def swap_chunks(rows, width):
@@ -50,44 +53,58 @@
     return lax.dot_general(a, b, ((contract[:1], contract[1:]), ((), ())), preferred_element_type=F32)
 
 
-def filter_kernel(map_ref, v0_ref, v1_ref, v2_ref, v3_ref, fir_ref, cos_ref, sin_ref, out_ref, w_ref, acc_ref):
-    step = pl.program_id(0)
-
-    @pl.when(step == 0)
-    def _():
-        halves = []
-        for p in range(2):
+def prepare_kernel(map_hbm, volts_hbm, fir_hbm, table_hbm, own_ref, fir_ref, table_ref, tiles_ref, map_ref, volts_ref, sems):
+    copies = [
+        pltpu.make_async_copy(volts_hbm.at[0], volts_ref, sems.at[0]),
+        pltpu.make_async_copy(fir_hbm, fir_ref, sems.at[1]),
+        pltpu.make_async_copy(table_hbm, table_ref, sems.at[2]),
+        pltpu.make_async_copy(map_hbm, map_ref, sems.at[3]),
+    ]
+    for copy in copies:
+        copy.start()
+    copies[0].wait()
+    own_ref[...] = volts_ref[...].astype(F32).astype(BF)
+    own = (lax.axis_index("x") * ZR + lax.axis_index("zr")) * C + lax.axis_index("c")
+    copies[3].wait()
+    sub = lax.broadcasted_iota(jnp.int32, (8, LANES), 0)
+    place = lax.broadcasted_iota(jnp.int32, (8, LANES), 1) + (sub % 2) * LANES - own * SLOT
+    tiles = jnp.zeros((8, LANES), jnp.int32)
+    for l in range(OWN):
+        tiles = jnp.where(place == l, jnp.where(sub < 2, map_ref[0, l], map_ref[1, l]), tiles)
+    tiles_ref[...] = jnp.where(sub < 4, tiles, 0).astype(F32)
+    copies[1].wait()
+    copies[2].wait()
+
+
+def filter_kernel(v0_ref, v1_ref, v2_ref, v3_ref, fir_ref, table_ref, tiles_ref, out_ref):
+    re, im = [], []
+    for p, parts in enumerate((re, im)):
+        for q in range(4):
+            at = q * QUARTER
             total = None
             for k, ref in enumerate((v0_ref, v1_ref, v2_ref, v3_ref)):
-                part = ref[:, p * NCHAN : (p + 1) * NCHAN].astype(F32) * 0.25
-                term = fir_ref[k : k + 1, :] * part
+                part = ref[:, p * NCHAN + at : p * NCHAN + at + QUARTER].astype(F32) * 0.25
+                term = fir_ref[k : k + 1, at : at + QUARTER] * part
                 total = term if total is None else total + term
-            halves.append(total.astype(BF).astype(F32))
-        re, im = halves
-        w_ref[0] = jnp.concatenate([re, im] * 4, axis=0).astype(BF)
-        w_ref[1] = jnp.concatenate([im, -re] * 4, axis=0).astype(BF)
-        acc_ref[...] = jnp.zeros_like(acc_ref)
-
-    block = lax.broadcasted_iota(jnp.int32, (LANES, NCHAN), 0) // 32
-    here = block == step
-    total = acc_ref[...]
-    for i, ref in enumerate((cos_ref, sin_ref)):
-        weights = jnp.where(here, w_ref[i].astype(F32), 0.0).astype(BF)
-        total = total + dot(ref[0], weights, (1, 1))
-    acc_ref[...] = total
-
-    @pl.when(step == pl.num_programs(0) - 1)
-    def _():
-        own = (lax.axis_index("x") * ZR + lax.axis_index("zr")) * C + lax.axis_index("c")
-        sub = lax.broadcasted_iota(jnp.int32, (8, LANES), 0)
-        place = lax.broadcasted_iota(jnp.int32, (8, LANES), 1) + (sub % 2) * LANES - own * 16
-        tiles = jnp.zeros((8, LANES), jnp.int32)
-        for l in range(OWN):
-            tiles = jnp.where(place == l, jnp.where(sub < 2, map_ref[0, l], map_ref[1, l]), tiles)
-        tiles = jnp.where(sub < 4, tiles, 0).astype(F32)
-        data = acc_ref[...].reshape(Y * X, 8, LANES)
-        both = jnp.concatenate([data, jnp.broadcast_to(tiles[None], data.shape)], axis=1)
-        out_ref[...] = both.astype(BF)
+            parts.append(total.astype(BF).astype(F32))
+    evens = [(x[0] + x[2], x[1] + x[3]) for x in (re, im)]
+    odds = [(x[0] - x[2], x[1] - x[3]) for x in (re, im)]
+    sums = (
+        (evens[0][0] + evens[0][1], evens[1][0] + evens[1][1]),
+        (odds[0][0] + odds[1][1], odds[1][0] - odds[0][1]),
+        (evens[0][0] - evens[0][1], evens[1][0] - evens[1][1]),
+        (odds[0][0] - odds[1][1], odds[1][0] + odds[0][1]),
+    )
+    total = None
+    for j, (r, m) in enumerate(sums):
+        live = jnp.concatenate([jnp.concatenate([r, m], axis=1), jnp.concatenate([m, -r], axis=1)], axis=0).astype(BF)
+        rows = [jnp.zeros((32, 2 * QUARTER), BF)] * 4
+        rows[j] = live
+        part = dot(table_ref[:, j * 2 * QUARTER : (j + 1) * 2 * QUARTER], jnp.concatenate(rows, axis=0), (1, 1))
+        total = part if total is None else total + part
+    data = total.reshape(Y * X, 8, LANES)
+    both = jnp.concatenate([data, jnp.broadcast_to(tiles_ref[...][None], data.shape)], axis=1)
+    out_ref[...] = both.astype(BF)
 
 
 def turn_kernel(in_ref, out_ref, f_ref):
@@ -135,40 +152,47 @@
     rh, sh = jnp.where(r >= 16, 1, 0), jnp.where(s >= 16, 1, 0)
     index = (rh + sh) * 256 + (s - 16 * sh) * 16 + (r - 16 * rh)
     pick = jnp.where(lax.broadcasted_iota(jnp.int32, (768, 256), 0) == index, 1.0, 0.0).astype(BF)
-    picked = dot(pick, d_ref[...], (0, 0)).astype(BF)
+    c_ref[: 16 * SLOT, :] = dot(pick, d_ref[:, :256], (0, 0))[: 16 * SLOT]
+    c_ref[256 : 256 + 16 * SLOT, :] = dot(pick, d_ref[:, 256:], (0, 0))[: 16 * SLOT]
     for d in range(16):
         for ch in range(4):
-            out_ref[d, ch * 16 : (ch + 1) * 16, :] = picked[d * 16 : (d + 1) * 16, ch * LANES : (ch + 1) * LANES]
+            rows = c_ref[(ch // 2) * 256 + d * SLOT : (ch // 2) * 256 + (d + 1) * SLOT, (ch % 2) * LANES : (ch % 2 + 1) * LANES]
+            f_ref[d * 48 + ch * SLOT : d * 48 + (ch + 1) * SLOT, :] = rows
+    out_ref[...] = f_ref[: 16 * 48, :].reshape(16, 48, LANES).astype(BF)
 
 
 def place_kernel(in_ref, out_ref, f_ref):
     f_ref[...] = in_ref[...].astype(F32).reshape(f_ref.shape)
     for l in range(OWN):
-        out_ref[l] = f_ref[pl.ds(l, 64, stride=16), :]
+        out_ref[l] = f_ref[pl.ds(l, 64, stride=SLOT), :]
 
 
 PARAMS = pltpu.CompilerParams(vmem_limit_bytes=VMEM)
 
 
 def per_device(voltages, fir_taps, tile_map):
-    own = voltages[0].astype(BF)
+    hbm = pl.BlockSpec(memory_space=pltpu.MemorySpace.HBM)
+    own, fir, table, tiles = pl.pallas_call(
+        prepare_kernel,
+        out_shape=(
+            jax.ShapeDtypeStruct((16, 2 * NCHAN), BF),
+            jax.ShapeDtypeStruct((4, NCHAN), F32),
+            jax.ShapeDtypeStruct((256, 8 * QUARTER), BF),
+            jax.ShapeDtypeStruct((8, LANES), F32),
+        ),
+        in_specs=[hbm] * 4,
+        scratch_shapes=[pltpu.SMEM((2, OWN), jnp.int32), pltpu.VMEM((16, 2 * NCHAN), jnp.int32), pltpu.SemaphoreType.DMA((4,))],
+        compiler_params=PARAMS,
+        name="prepare",
+    )(*(pltpu.with_memory_space_constraint(a, pltpu.MemorySpace.HBM) for a in (tile_map.T, voltages, fir_taps, jnp.asarray(dft_table()))))
     count = X * ZQ * ZR * C
     before = [lax.ppermute(own, TILE_AXES, [(t, t + k) for t in range(count - k)]) for k in (1, 2, 3)]
-    cos, sin = dft_tables()
-    whole = lambda *shape: pl.BlockSpec(shape, lambda j: (0,) * len(shape))
-    table = pl.BlockSpec((1, 256, NCHAN), lambda j: (j, 0, 0))
     sent = pl.pallas_call(
         filter_kernel,
         out_shape=jax.ShapeDtypeStruct((Y * X, 16, LANES), BF),
-        grid=(4,),
-        in_specs=[pl.BlockSpec(memory_space=pltpu.SMEM)]
-        + [whole(16, 2 * NCHAN)] * 4
-        + [whole(4, NCHAN), table, table],
-        out_specs=whole(Y * X, 16, LANES),
-        scratch_shapes=[pltpu.VMEM((2, LANES, NCHAN), BF), pltpu.VMEM((256, LANES), F32)],
         compiler_params=PARAMS,
         name="filter",
-    )(tile_map.T, own, *before, fir_taps, jnp.asarray(cos), jnp.asarray(sin))
+    )(own, *before, fir, table, tiles)
     came = lax.all_to_all(sent, ("y", "x"), 0, 0, tiled=True)
     sent = pl.pallas_call(
         turn_kernel,
@@ -180,7 +204,7 @@
     came = lax.all_to_all(sent, ("zh", "zq", "zr", "c"), 0, 0, tiled=True)
     sent = pl.pallas_call(
         correlate_kernel,
-        out_shape=jax.ShapeDtypeStruct((16, 64, LANES), BF),
+        out_shape=jax.ShapeDtypeStruct((16, 4 * SLOT, LANES), BF),
         scratch_shapes=[
             pltpu.VMEM((1024, LANES), F32),
             pltpu.VMEM((4, LANES, 256), BF),
@@ -194,7 +218,7 @@
     return pl.pallas_call(
         place_kernel,
         out_shape=jax.ShapeDtypeStruct((OWN, 64, LANES), F32),
-        scratch_shapes=[pltpu.VMEM((1024, LANES), F32)],
+        scratch_shapes=[pltpu.VMEM((16 * 4 * SLOT, LANES), F32)],
         compiler_params=PARAMS,
         name="place",
     )(came)

time: 92.1 us -> 85.3 us (0.926)
  local copies, waits for them, and re-layouts: 4.58 us -> 0 us
    unnamed x8 -> x0, local copies, waits for them, and re-layouts: 4.58 us -> none
    pallas_call x1, Pallas kernels: 2.58 us -> 0.49 us  [per_device(): pl.pallas_call(filter_kernel, out_shape=jax.ShapeDtypeStruct((Y * X, 16,...]
    pallas_call x1 -> x2, Pallas kernels: 2.41 us -> 3.77 us  [the longest x1 2.42 us: per_device(): pl.pallas_call(correlate_kernel, out_shape=jax.ShapeDtypeStruct((16, 4 *...]
where the time goes in v2:
time: 85.3 us; the launch traced here: 85 us
  blocking collectives  64.6 us (76%)
  starting transfers between devices  13.4 us (16%)
  Pallas kernels  5.15 us (6%)
  waiting for transfers between devices  1.84 us (2%)
    all_to_all x1, blocking collectives, per_device(): came = lax.all_to_all(sent, ('zh', 'zq', 'zr', 'c'), 0, 0, tiled=True)  31.9 us
    all_to_all x1, blocking collectives, per_device(): came = lax.all_to_all(sent, ('y', 'x'), 0, 0, tiled=True)  22.2 us
    ppermute x3, starting transfers between devices, per_device(): lax.ppermute(own, TILE_AXES, [(t, t + k) for t in range(count - k)])  13.4 us
    all_to_all x1, blocking collectives, per_device(): came = lax.all_to_all(sent, ('x', 'zr', 'c'), 0, 0, tiled=True)  10.5 us
    pallas_call x1, Pallas kernels, per_device(): pl.pallas_call(correlate_kernel, out_shape=jax.ShapeDtypeStruct((16, 4 *...  2.42 us
    ppermute x3, waiting for transfers between devices, per_device(): lax.ppermute(own, TILE_AXES, [(t, t + k) for t in range(count - k)])  1.84 us
  transfers between devices with their start and end apart: 3, of which 1 were waited for; matrix products, arithmetic and copies ran while one was open for 0% of the time, Pallas kernels for 0%

profile of v2, /device:TPU:1, one launch (start us, length us, event | category | flops | bytes accessed | tf_op | source)
XLA Modules:
  0.0 85.0 jit_solution(10569287885473476434)
XLA Ops:
  0.0 1.4 %prepare.1 = (bf16[16,2048]{1,0:T(8,128)(2,1)S(1)}, f32[4,1024]{1,0:T(4,128)S(1)}, bf16[256,2048]{1,0:T(8,128)(2,1)S(1)}, f32[8,128]{1,0:T(8,128)S(1)}) custom-call(s32[2,11]{1,0:T(2,128)} %bitcast.1, s32[1,16,2048]{2,1,0:T(8,128)} %volts_hbm.1, f32[4,1024]{1,0:T(4,128)} %fir_hbm.1, bf16[256,2048]{1,0:T(8,128)(2,1)} %constant.2.clone.table_hbm), custom_call_target="tpu_custom_call" | custom-call | tf_op jit(solution)/shard_map/prepare/pallas_call | solution.py:175
  1.4 7.2 %collective-permute-start.2 = (bf16[16,2048]{1,0:T(8,128)(2,1)S(1)}, bf16[16,2048]{1,0:T(8,128)(2,1)S(1)}, u32[]{:S(2)}, u32[]{:S(2)}) collective-permute-start(bf16[16,2048]{1,0:T(8,128)(2,1)S(1)} %get-tuple-element.9.v0_ref), channel_id=1, source_target_pairs={{0,3},{1,4},{2,5},{3,6},{4,7},{5,8},{6,9},{7,10},{8,11},{9,12},{10... | collective-permute-start | bytes 196616 | tf_op jit(solution)/shard_map/ppermute | solution.py:189
  8.6 4.0 %collective-permute-start.1 = (bf16[16,2048]{1,0:T(8,128)(2,1)S(1)}, bf16[16,2048]{1,0:T(8,128)(2,1)S(1)}, u32[]{:S(2)}, u32[]{:S(2)}) collective-permute-start(bf16[16,2048]{1,0:T(8,128)(2,1)S(1)} %get-tuple-element.9.v0_ref), channel_id=1, source_target_pairs={{0,2},{1,3},{2,4},{3,5},{4,6},{5,7},{6,8},{7,9},{8,10},{9,11},{10,... | collective-permute-start | bytes 196616 | tf_op jit(solution)/shard_map/ppermute | solution.py:189
  12.6 2.2 %collective-permute-start = (bf16[16,2048]{1,0:T(8,128)(2,1)S(1)}, bf16[16,2048]{1,0:T(8,128)(2,1)S(1)}, u32[]{:S(2)}, u32[]{:S(2)}) collective-permute-start(bf16[16,2048]{1,0:T(8,128)(2,1)S(1)} %get-tuple-element.9.v0_ref), channel_id=1, source_target_pairs={{0,1},{1,2},{2,3},{3,4},{4,5},{5,6},{6,7},{7,8},{8,9},{9,10},{10,1... | collective-permute-start | bytes 196616 | tf_op jit(solution)/shard_map/ppermute | solution.py:189
  14.8 0.0 collective-permute-done.2.v3_ref
  14.8 0.0 collective-permute-done.1.v2_ref
  14.8 1.8 %collective-permute-done.v1_ref = bf16[16,2048]{1,0:T(8,128)(2,1)S(1)} collective-permute-done((bf16[16,2048]{1,0:T(8,128)(2,1)S(1)}, bf16[16,2048]{1,0:T(8,128)(2,1)S(1)}, u32[]{:S(2)}, u32[]{:S(2)}) %collective-permute-start) | collective-permute-done | bytes 65568 | tf_op jit(solution)/shard_map/ppermute | solution.py:189
  16.6 0.5 filter.1
  17.1 22.2 %all_to_all.15.in_ref = bf16[32,16,128]{2,1,0:T(8,128)(2,1)S(1)} all-to-all(bf16[32,16,128]{2,1,0:T(8,128)(2,1)S(1)} %filter.1), channel_id=1, replica_groups=mesh['zh'=2,'y'=8,'x'=4,'zq'=3,'zr'=2,'c'=2] {'y','x'}, dimensions={0} | all-to-all | bytes 262144 | tf_op jit(solution)/shard_map/all_to_all | solution.py:196
  39.3 0.1 turn.1
  39.4 31.9 %all_to_all.16.in_ref = bf16[24,40,128]{2,1,0:T(8,128)(2,1)S(1)} all-to-all(bf16[24,40,128]{2,1,0:T(8,128)(2,1)S(1)} %turn.1), channel_id=1, replica_groups=mesh['zh'=2,'y'=8,'x'=4,'zq'=3,'zr'=2,'c'=2] {'zh','zq','zr','c'}, dimensions={0} | all-to-all | bytes 491520 | tf_op jit(solution)/shard_map/all_to_all | solution.py:204
  71.3 2.4 %correlate.1 = bf16[16,48,128]{2,1,0:T(8,128)(2,1)S(1)} custom-call(bf16[24,40,128]{2,1,0:T(8,128)(2,1)S(1)} %all_to_all.16.in_ref), custom_call_target="tpu_custom_call" | custom-call | tf_op jit(solution)/shard_map/correlate/pallas_call | solution.py:205
  73.7 10.5 %all_to_all.17.in_ref = bf16[16,48,128]{2,1,0:T(8,128)(2,1)S(1)} all-to-all(bf16[16,48,128]{2,1,0:T(8,128)(2,1)S(1)} %correlate.1), channel_id=1, replica_groups=mesh['zh'=2,'y'=8,'x'=4,'zq'=3,'zr'=2,'c'=2] {'x','zr','c'}, dimensions={0} | all-to-all | bytes 393216 | tf_op jit(solution)/shard_map/all_to_all | solution.py:217
  84.2 0.8 place.1
Async XLA Ops:
  1.4 13.4 %collective-permute-start.2 = (bf16[16,2048]{1,0:T(8,128)(2,1)S(1)}, bf16[16,2048]{1,0:T(8,128)(2,1)S(1)}, u32[]{:S(2)}, u32[]{:S(2)}) collective-permute-start(bf16[16,2048]{1,0:T(8,128)(2,1)S(1)} %get-tuple-element.9.v0_ref), channel_id=1, source_target_pairs={{0,3},{1,4},{2,5},{3,6},{4,7},{5,8},{6,9},{7,10},{8,11},{9,12},{10... | collective-permute-start | bytes 196616 | tf_op jit(solution)/shard_map/ppermute | solution.py:189
  8.6 6.2 %collective-permute-start.1 = (bf16[16,2048]{1,0:T(8,128)(2,1)S(1)}, bf16[16,2048]{1,0:T(8,128)(2,1)S(1)}, u32[]{:S(2)}, u32[]{:S(2)}) collective-permute-start(bf16[16,2048]{1,0:T(8,128)(2,1)S(1)} %get-tuple-element.9.v0_ref), channel_id=1, source_target_pairs={{0,2},{1,3},{2,4},{3,5},{4,6},{5,7},{6,8},{7,9},{8,10},{9,11},{10,... | collective-permute-start | bytes 196616 | tf_op jit(solution)/shard_map/ppermute | solution.py:189
  12.6 4.1 %collective-permute-start = (bf16[16,2048]{1,0:T(8,128)(2,1)S(1)}, bf16[16,2048]{1,0:T(8,128)(2,1)S(1)}, u32[]{:S(2)}, u32[]{:S(2)}) collective-permute-start(bf16[16,2048]{1,0:T(8,128)(2,1)S(1)} %get-tuple-element.9.v0_ref), channel_id=1, source_target_pairs={{0,1},{1,2},{2,3},{3,4},{4,5},{5,6},{6,7},{7,8},{8,9},{9,10},{10,1... | collective-permute-start | bytes 196616 | tf_op jit(solution)/shard_map/ppermute | solution.py:189

commit v3 on v2

v3 whole, which is shorter than its diff:
```python
import math

import jax
import jax.numpy as jnp
import ml_dtypes
import numpy as np
from jax import lax
from jax.experimental import pallas as pl
from jax.experimental.pallas import tpu as pltpu
from jax.sharding import Mesh, PartitionSpec as P

NCHAN = 1024
QUARTER = NCHAN // 4
TIME = 48
TAPS = 4
FRAMES = 4 + TAPS - 1
LANES = 128
ZH, Y, X, ZQ, ZR, C = 2, 8, 4, 3, 2, 2
TILE_AXES = ("x", "zq", "zr", "c")
OWN = 11
SLOT = 12
VMEM = 48 * 1024 * 1024

BF = jnp.bfloat16
F32 = jnp.float32


def dft_table():
    zr, c, zh, x, y = np.meshgrid(*(np.arange(n) for n in (ZR, C, ZH, X, Y)), indexing="ij")
    first = ((zh * Y + y) * 64 + ((x * ZR + zr) * C + c) * 4).reshape(-1)
    channels = first[:, None] + np.arange(4)[None, :]
    products = channels[:, :, None] * np.arange(QUARTER)[None, None, :] % NCHAN
    angles = products.astype(np.float32) * np.float32(2.0 * math.pi / NCHAN)
    scale = np.float32(1.0 / math.sqrt(NCHAN))
    both = np.stack([np.cos(angles) * scale, np.sin(angles) * scale], axis=2)
    return both.reshape(256, 8 * QUARTER).astype(ml_dtypes.bfloat16)


def swap_chunks(rows, width):
    rows = list(rows)
    chunk = lax.broadcasted_iota(jnp.int32, rows[0].shape, 1) // width
    step = len(rows) // 2
    while step:
        low = (chunk & step) == 0
        for g in range(len(rows)):
            if not g & step:
                a, b = rows[g], rows[g + step]
                rows[g] = jnp.where(low, a, pltpu.roll(b, step * width, 1))
                rows[g + step] = jnp.where(low, pltpu.roll(a, LANES - step * width, 1), b)
        step //= 2
    return rows


def dot(a, b, contract):
    return lax.dot_general(a, b, ((contract[:1], contract[1:]), ((), ())), preferred_element_type=F32)


def split(value):
    high = value.astype(BF)
    return high, (value - high.astype(F32)).astype(BF)


def tap_kernel(map_hbm, volts_hbm, fir_hbm, table_hbm, out_ref, map_ref, volts_ref, fir_ref, table_ref, sems):
    pairs = ((volts_hbm.at[0], volts_ref), (fir_hbm, fir_ref), (map_hbm, map_ref), (table_hbm, table_ref))
    copies = [pltpu.make_async_copy(src, dst, sems.at[i]) for i, (src, dst) in enumerate(pairs)]
    for copy in copies:
        copy.start()
    copies[0].wait()
    copies[1].wait()
    lives = [[] for _ in range(4)]
    for k in range(TAPS):
        re, im = [], []
        for p, parts in enumerate((re, im)):
            for q in range(4):
                at = q * QUARTER
                part = volts_ref[:, p * NCHAN + at : p * NCHAN + at + QUARTER].astype(F32) * 0.25
                parts.append(fir_ref[k : k + 1, at : at + QUARTER] * part)
        evens = [(v[0] + v[2], v[1] + v[3]) for v in (re, im)]
        odds = [(v[0] - v[2], v[1] - v[3]) for v in (re, im)]
        sums = (
            (evens[0][0] + evens[0][1], evens[1][0] + evens[1][1]),
            (odds[0][0] + odds[1][1], odds[1][0] - odds[0][1]),
            (evens[0][0] - evens[0][1], evens[1][0] - evens[1][1]),
            (odds[0][0] - odds[1][1], odds[1][0] + odds[0][1]),
        )
        for j, (r, m) in enumerate(sums):
            lives[j] += [jnp.concatenate([r, m], axis=1), jnp.concatenate([m, -r], axis=1)]
    copies[3].wait()
    outs = []
    for j in range(4):
        table = table_ref[:, j * 2 * QUARTER : (j + 1) * 2 * QUARTER]
        high, low = split(jnp.concatenate(lives[j], axis=0))
        outs.append(dot(table, high, (1, 1)) + dot(table, low, (1, 1)))
    for k, part in enumerate(swap_chunks(outs, 32)):
        for j in range(ZR * C):
            out_ref[j, k * 64 : (k + 1) * 64, :] = part[j * 64 : (j + 1) * 64].astype(BF)

    copies[2].wait()
    sub = lax.broadcasted_iota(jnp.int32, (8, LANES), 0)
    lane = lax.broadcasted_iota(jnp.int32, (8, LANES), 1)
    place = lane - (lax.axis_index("zr") * C + lax.axis_index("c")) * SLOT
    tiles = jnp.zeros((8, LANES), jnp.int32)
    for l in range(OWN):
        tiles = jnp.where(place == l, map_ref[0, l], tiles)
        tiles = jnp.where(place == l + 64, map_ref[1, l], tiles)
    tiles = jnp.where(sub == 0, tiles, 0).astype(F32).astype(BF)
    for j in range(ZR * C):
        out_ref[j, 256:264, :] = tiles


def sum_kernel(in_ref, out_ref, f_ref):
    for f in range(FRAMES):
        total = None
        for k in range(TAPS):
            if 0 <= f - k < 4:
                part = in_ref[f - k, k * 64 : (k + 1) * 64, :].astype(F32)
                total = part if total is None else total + part
        for zh in range(ZH):
            f_ref[pl.ds(zh * FRAMES + f, X * Y, stride=16), :] = total[zh * X * Y : (zh + 1) * X * Y]
    tiles = sum(in_ref[j, 256:264, :].astype(F32) for j in range(ZR * C))
    f_ref[pl.ds(14, X * Y, stride=16), :] = jnp.broadcast_to(tiles[0:1], (X * Y, LANES))
    f_ref[pl.ds(15, X * Y, stride=16), :] = jnp.zeros((X * Y, LANES), F32)
    out_ref[...] = f_ref[...].reshape(X * Y, 16, LANES).astype(BF)


def turn_kernel(in_ref, out_ref, tiles_ref, f_ref):
    f_ref[...] = in_ref[...].astype(F32).reshape(f_ref.shape)
    for zh in range(ZH):
        for f in range(FRAMES):
            rows = f_ref[pl.ds(zh * FRAMES + f, X * Y, stride=16), :].astype(BF)
            for zq in range(ZQ):
                out_ref[zh * ZQ + zq, f * X * Y : (f + 1) * X * Y, :] = rows
    tiles_ref[...] = f_ref[pl.ds(14, X, stride=16 * Y), :]


def correlate_kernel(in_ref, tiles_ref, out_ref, f_ref, a_ref, c_ref, d_ref):
    def part(zh, zq, f):
        return in_ref[zh * ZQ + zq, f * 32 : (f + 1) * 32, :].astype(F32)

    for zh in range(ZH):
        for zq in range(ZQ):
            for f in range(4):
                rows = part(zh, zq, f)
                if f + 4 < FRAMES:
                    if zq:
                        rows = rows + part(zh, zq - 1, f + 4)
                    else:
                        spill = part(zh, ZQ - 1, f + 4)
                        rows = rows + jnp.concatenate([jnp.zeros((Y, LANES), F32), spill[: 32 - Y]], axis=0)
                f_ref[((zh * ZQ + zq) * 4 + f) * 32 : ((zh * ZQ + zq) * 4 + f + 1) * 32, :] = rows
    for zh in range(ZH):
        groups = [f_ref[pl.ds(zh * 384 + y, TIME, stride=Y), :] for y in range(Y)]
        for k, rows in enumerate(swap_chunks(groups, 16)):
            ch, p = divmod(k, 2)
            a_ref[ch, p * TIME : (p + 1) * TIME, zh * LANES : (zh + 1) * LANES] = rows.astype(BF)

    i = lax.broadcasted_iota(jnp.int32, (256, 256), 0)
    j = lax.broadcasted_iota(jnp.int32, (256, 256), 1)
    order = jnp.where(i == (j % 32) * 8 + j // 32, 1.0, 0.0).astype(BF)
    for ch in range(4):
        cols = a_ref[ch]
        left = dot(cols, order, (1, 0))
        re, im = left[:TIME], left[TIME:]
        both = jnp.concatenate([jnp.concatenate([re, im], axis=0), jnp.concatenate([im, -re], axis=0)], axis=1)
        c_ref[...] = dot(both.astype(BF), cols, (0, 0)) * (1.0 / TIME)
        for block, (h, g) in enumerate(((0, 0), (1, 0), (1, 1))):
            rows = [c_ref[k * 32 + g * 16 : k * 32 + g * 16 + 16, h * LANES : (h + 1) * LANES] for k in range(16)]
            for s, part in enumerate(swap_chunks(rows, 8)):
                at = block * 256 + s * 16
                d_ref[at : at + 16, ch * LANES : (ch + 1) * LANES] = part.astype(BF)

    lane = lax.broadcasted_iota(jnp.int32, (8, LANES), 1)
    firsts, seconds = [], []
    for half in range(2):
        for shift, found in ((0, firsts), (64, seconds)):
            total = None
            for x in range(2):
                rows = jnp.broadcast_to(tiles_ref[half * 2 + x : half * 2 + x + 1, :], (8, LANES))
                rows = pltpu.roll(rows, shift, 1) if shift else rows
                rows = jnp.where(lane < 4 * SLOT, rows, 0.0)
                total = rows if total is None else total + pltpu.roll(rows, x * 4 * SLOT, 1)
            found.append(total[0:1])
    r = jnp.concatenate(firsts, axis=1).astype(jnp.int32)
    s = jnp.concatenate(seconds, axis=1).astype(jnp.int32)
    rh, sh = jnp.where(r >= 16, 1, 0), jnp.where(s >= 16, 1, 0)
    index = (rh + sh) * 256 + (s - 16 * sh) * 16 + (r - 16 * rh)
    pick = jnp.where(lax.broadcasted_iota(jnp.int32, (768, 256), 0) == index, 1.0, 0.0).astype(BF)
    c_ref[:256, :] = dot(pick, d_ref[:, :256], (0, 0))
    c_ref[256:, :] = dot(pick, d_ref[:, 256:], (0, 0))
    for d in range(16):
        for ch in range(4):
            at = (ch // 2) * 256 + (d // 8) * LANES + (d % 8) * SLOT
            rows = c_ref[at : at + SLOT, (ch % 2) * LANES : (ch % 2 + 1) * LANES]
            f_ref[d * 48 + ch * SLOT : d * 48 + (ch + 1) * SLOT, :] = rows
    out_ref[...] = f_ref[...].reshape(16, 48, LANES).astype(BF)


def place_kernel(in_ref, out_ref, f_ref):
    f_ref[...] = in_ref[...].astype(F32).reshape(f_ref.shape)
    for l in range(OWN):
        out_ref[l] = f_ref[pl.ds(l, 64, stride=SLOT), :]


PARAMS = pltpu.CompilerParams(vmem_limit_bytes=VMEM)


def per_device(voltages, fir_taps, tile_map):
    hbm = pl.BlockSpec(memory_space=pltpu.MemorySpace.HBM)
    arrays = (tile_map.T, voltages, fir_taps, jnp.asarray(dft_table()))
    sent = pl.pallas_call(
        tap_kernel,
        out_shape=jax.ShapeDtypeStruct((ZR * C, 264, LANES), BF),
        in_specs=[hbm] * 4,
        scratch_shapes=[
            pltpu.SMEM((2, OWN), jnp.int32),
            pltpu.VMEM((16, 2 * NCHAN), jnp.int32),
            pltpu.VMEM((TAPS, NCHAN), F32),
            pltpu.VMEM((256, 8 * QUARTER), BF),
            pltpu.SemaphoreType.DMA((4,)),
        ],
        compiler_params=PARAMS,
        name="taps",
    )(*(pltpu.with_memory_space_constraint(a, pltpu.MemorySpace.HBM) for a in arrays))
    came = lax.all_to_all(sent, ("zr", "c"), 0, 0, tiled=True)
    sent = pl.pallas_call(
        sum_kernel,
        out_shape=jax.ShapeDtypeStruct((X * Y, 16, LANES), BF),
        scratch_shapes=[pltpu.VMEM((X * Y * 16, LANES), F32)],
        compiler_params=PARAMS,
        name="sum",
    )(came)
    came = lax.all_to_all(sent, ("x", "y"), 0, 0, tiled=True)
    sent, tiles = pl.pallas_call(
        turn_kernel,
        out_shape=(
            jax.ShapeDtypeStruct((ZH * ZQ, FRAMES * X * Y, LANES), BF),
            jax.ShapeDtypeStruct((X, LANES), F32),
        ),
        scratch_shapes=[pltpu.VMEM((X * Y * 16, LANES), F32)],
        compiler_params=PARAMS,
        name="turn",
    )(came)
    came = lax.all_to_all(sent, ("zh", "zq"), 0, 0, tiled=True)
    sent = pl.pallas_call(
        correlate_kernel,
        out_shape=jax.ShapeDtypeStruct((16, 4 * SLOT, LANES), BF),
        scratch_shapes=[
            pltpu.VMEM((768, LANES), F32),
            pltpu.VMEM((4, 2 * TIME, 256), BF),
            pltpu.VMEM((512, 256), F32),
            pltpu.VMEM((768, 512), BF),
        ],
        compiler_params=PARAMS,
        name="correlate",
    )(came, tiles)
    came = lax.all_to_all(sent, ("x", "zr", "c"), 0, 0, tiled=True)
    return pl.pallas_call(
        place_kernel,
        out_shape=jax.ShapeDtypeStruct((OWN, 64, LANES), F32),
        scratch_shapes=[pltpu.VMEM((16 * 4 * SLOT, LANES), F32)],
        compiler_params=PARAMS,
        name="place",
    )(came)


def solution(mesh):
    fine = Mesh(mesh.devices.reshape(ZH, Y, X, ZQ, ZR, C), ("zh", "y") + TILE_AXES)
    in_specs = (P(TILE_AXES, ("zh", "y"), None), P(), P(TILE_AXES, None))
    out_specs = P(TILE_AXES, ("zh", "y"), None)
    return jax.shard_map(per_device, mesh=fine, in_specs=in_specs, out_specs=out_specs, check_vma=False)
```

time: 85.3 us -> 76.3 us (0.89)
  starting transfers between devices: 13.4 us -> 0 us
  blocking collectives: 64.6 us -> 70.2 us
  waiting for transfers between devices: 1.84 us -> 0 us
    ppermute x3 -> x0, starting transfers between devices: 13.4 us -> none  [per_device(): lax.ppermute(own, TILE_AXES, [(t, t + k) for t in range(count - k)])]
    all_to_all x2 -> x3, blocking collectives: 54 us -> 57.7 us  [the longest x1 27 us: per_device(): came = lax.all_to_all(sent, ('zh', 'zq'), 0, 0, tiled=True)]
    all_to_all x1, blocking collectives: 10.5 us -> 12.5 us  [per_device(): came = lax.all_to_all(sent, ('x', 'zr', 'c'), 0, 0, tiled=True)]
    ppermute x3 -> x0, waiting for transfers between devices: 1.84 us -> none  [per_device(): lax.ppermute(own, TILE_AXES, [(t, t + k) for t in range(count - k)])]
  transfers between devices with their start and end apart: 3 -> 0, of which waited for: 1 -> 0; matrix products, arithmetic and copies ran while one was open for 0% -> 0% of each run, Pallas kernels for 0% -> 0%
where the time goes in v3:
time: 76.3 us; the launch traced here: 76 us
  blocking collectives  70.2 us (92%)
  Pallas kernels  5.77 us (8%)
    all_to_all x1, blocking collectives, per_device(): came = lax.all_to_all(sent, ('zh', 'zq'), 0, 0, tiled=True)  27 us
    all_to_all x1, blocking collectives, per_device(): came = lax.all_to_all(sent, ('zr', 'c'), 0, 0, tiled=True)  18.6 us
    all_to_all x1, blocking collectives, per_device(): came = lax.all_to_all(sent, ('x', 'zr', 'c'), 0, 0, tiled=True)  12.5 us
    all_to_all x1, blocking collectives, per_device(): came = lax.all_to_all(sent, ('x', 'y'), 0, 0, tiled=True)  12.1 us
    pallas_call x1, Pallas kernels, per_device(): pl.pallas_call(correlate_kernel, out_shape=jax.ShapeDtypeStruct((16, 4 *...  2.5 us
    pallas_call x1, Pallas kernels, per_device(): pl.pallas_call(tap_kernel, out_shape=jax.ShapeDtypeStruct((ZR * C, 264, L...  2.26 us

profile of v3, /device:TPU:1, one launch (start us, length us, event | category | flops | bytes accessed | tf_op | source)
XLA Modules:
  0.0 76.0 jit_solution(11684350441332605382)
XLA Ops:
  0.0 2.3 %taps.1 = bf16[4,264,128]{2,1,0:T(8,128)(2,1)S(1)} custom-call(s32[2,11]{1,0:T(2,128)} %bitcast.1, s32[1,16,2048]{2,1,0:T(8,128)} %volts_hbm.1, f32[4,1024]{1,0:T(4,128)} %fir_hbm.1, bf16[256,2048]{1,0:T(8,128)(2,1)} %constant.2.clone.table_hbm), custom_call_target="tpu_custom_call" | custom-call | tf_op jit(solution)/shard_map/taps/pallas_call | solution.py:210
  2.3 18.6 %all_to_all.20.in_ref = bf16[4,264,128]{2,1,0:T(8,128)(2,1)S(1)} all-to-all(bf16[4,264,128]{2,1,0:T(8,128)(2,1)S(1)} %taps.1), channel_id=1, replica_groups=mesh['zh'=2,'y'=8,'x'=4,'zq'=3,'zr'=2,'c'=2] {'zr','c'}, dimensions={0} | all-to-all | bytes 540672 | tf_op jit(solution)/shard_map/all_to_all | solution.py:224
  20.9 0.1 sum.1
  21.0 12.1 %all_to_all.21.in_ref = bf16[32,16,128]{2,1,0:T(8,128)(2,1)S(1)} all-to-all(bf16[32,16,128]{2,1,0:T(8,128)(2,1)S(1)} %sum.1), channel_id=1, replica_groups=mesh['zh'=2,'y'=8,'x'=4,'zq'=3,'zr'=2,'c'=2] {'x','y'}, dimensions={0} | all-to-all | bytes 262144 | tf_op jit(solution)/shard_map/all_to_all | solution.py:232
  33.1 0.1 turn.1
  33.2 27.0 %all_to_all.22.in_ref = bf16[6,224,128]{2,1,0:T(8,128)(2,1)S(1)} all-to-all(bf16[6,224,128]{2,1,0:T(8,128)(2,1)S(1)} %get-tuple-element.7), channel_id=1, replica_groups=mesh['zh'=2,'y'=8,'x'=4,'zq'=3,'zr'=2,'c'=2] {'zh','zq'}, dimensions={0} | all-to-all | bytes 688128 | tf_op jit(solution)/shard_map/all_to_all | solution.py:243
  60.2 2.5 %correlate.1 = bf16[16,48,128]{2,1,0:T(8,128)(2,1)S(1)} custom-call(bf16[6,224,128]{2,1,0:T(8,128)(2,1)S(1)} %all_to_all.22.in_ref, f32[4,128]{1,0:T(4,128)S(1)} %get-tuple-element.8.tiles_ref), custom_call_target="tpu_custom_call" | custom-call | tf_op jit(solution)/shard_map/correlate/pallas_call | solution.py:244
  62.7 12.5 %all_to_all.23.in_ref = bf16[16,48,128]{2,1,0:T(8,128)(2,1)S(1)} all-to-all(bf16[16,48,128]{2,1,0:T(8,128)(2,1)S(1)} %correlate.1), channel_id=1, replica_groups=mesh['zh'=2,'y'=8,'x'=4,'zq'=3,'zr'=2,'c'=2] {'x','zr','c'}, dimensions={0} | all-to-all | bytes 393216 | tf_op jit(solution)/shard_map/all_to_all | solution.py:256
  75.2 0.8 %place.1 = f32[11,64,128]{2,1,0:T(8,128)} custom-call(bf16[16,48,128]{2,1,0:T(8,128)(2,1)S(1)} %all_to_all.23.in_ref), custom_call_target="tpu_custom_call" | custom-call | tf_op jit(solution)/shard_map/place/pallas_call | solution.py:257

commit v4 on v3

--- a/solution.py
+++ b/solution.py
@@ -26,7 +26,7 @@
 
 
 def dft_table():
-    zr, c, zh, x, y = np.meshgrid(*(np.arange(n) for n in (ZR, C, ZH, X, Y)), indexing="ij")
+    x, zr, c, zh, y = np.meshgrid(*(np.arange(n) for n in (X, ZR, C, ZH, Y)), indexing="ij")
     first = ((zh * Y + y) * 64 + ((x * ZR + zr) * C + c) * 4).reshape(-1)
     channels = first[:, None] + np.arange(4)[None, :]
     products = channels[:, :, None] * np.arange(QUARTER)[None, None, :] % NCHAN
@@ -92,62 +92,60 @@
         high, low = split(jnp.concatenate(lives[j], axis=0))
         outs.append(dot(table, high, (1, 1)) + dot(table, low, (1, 1)))
     for k, part in enumerate(swap_chunks(outs, 32)):
-        for j in range(ZR * C):
-            out_ref[j, k * 64 : (k + 1) * 64, :] = part[j * 64 : (j + 1) * 64].astype(BF)
+        out_ref[:, k * 16 : (k + 1) * 16, :] = part.astype(BF).reshape(16, 16, LANES)
 
     copies[2].wait()
     sub = lax.broadcasted_iota(jnp.int32, (8, LANES), 0)
     lane = lax.broadcasted_iota(jnp.int32, (8, LANES), 1)
-    place = lane - (lax.axis_index("zr") * C + lax.axis_index("c")) * SLOT
+    own = (lax.axis_index("x") * ZR + lax.axis_index("zr")) * C + lax.axis_index("c")
+    place = lane + (sub % 2) * (8 * SLOT) - own * SLOT
     tiles = jnp.zeros((8, LANES), jnp.int32)
     for l in range(OWN):
-        tiles = jnp.where(place == l, map_ref[0, l], tiles)
-        tiles = jnp.where(place == l + 64, map_ref[1, l], tiles)
-    tiles = jnp.where(sub == 0, tiles, 0).astype(F32).astype(BF)
-    for j in range(ZR * C):
-        out_ref[j, 256:264, :] = tiles
-
-
-def sum_kernel(in_ref, out_ref, f_ref):
-    for f in range(FRAMES):
-        total = None
-        for k in range(TAPS):
-            if 0 <= f - k < 4:
-                part = in_ref[f - k, k * 64 : (k + 1) * 64, :].astype(F32)
-                total = part if total is None else total + part
-        for zh in range(ZH):
-            f_ref[pl.ds(zh * FRAMES + f, X * Y, stride=16), :] = total[zh * X * Y : (zh + 1) * X * Y]
-    tiles = sum(in_ref[j, 256:264, :].astype(F32) for j in range(ZR * C))
-    f_ref[pl.ds(14, X * Y, stride=16), :] = jnp.broadcast_to(tiles[0:1], (X * Y, LANES))
-    f_ref[pl.ds(15, X * Y, stride=16), :] = jnp.zeros((X * Y, LANES), F32)
-    out_ref[...] = f_ref[...].reshape(X * Y, 16, LANES).astype(BF)
-
-
-def turn_kernel(in_ref, out_ref, tiles_ref, f_ref):
+        tiles = jnp.where(place == l, jnp.where(sub < 2, map_ref[0, l], map_ref[1, l]), tiles)
+    tiles = jnp.where((sub < 4) & (lane < 8 * SLOT), tiles, 0).astype(F32).astype(BF)
+    for d in range(16):
+        out_ref[d, 64:72, :] = tiles
+
+
+def sum_kernel(in_ref, out_ref, tiles_ref, f_ref):
+    zq = lax.axis_index("zq")
+    sums = [[None] * (FRAMES + 1) for _ in range(X)]
+    for x in range(X):
+        for f in range(FRAMES):
+            for k in range(TAPS):
+                if 0 <= f - k < 4:
+                    part = in_ref[x * 4 + f - k, k * 16 : (k + 1) * 16, :].astype(F32)
+                    sums[x][f] = part if sums[x][f] is None else sums[x][f] + part
+        sums[x][FRAMES] = jnp.zeros((16, LANES), F32)
+    zeros = jnp.zeros((16, LANES), F32)
+    for spill in range(2):
+        for x in range(X):
+            for f in range(4):
+                rows = sums[x][4 * spill + f]
+                if spill:
+                    rows = jnp.where(zq == ZQ - 1, sums[x - 1][4 + f] if x else zeros, rows)
+                for zh in range(ZH):
+                    at = spill * 256 + zh * 16 + x * 4 + f
+                    f_ref[pl.ds(at, Y, stride=32), :] = rows[zh * Y : (zh + 1) * Y]
+    out_ref[zq] = f_ref[:256, :].reshape(Y, 32, LANES).astype(BF)
+    out_ref[lax.rem(zq + 1, ZQ)] = f_ref[256:, :].reshape(Y, 32, LANES).astype(BF)
+    out_ref[lax.rem(zq + 2, ZQ)] = jnp.zeros((Y, 32, LANES), BF)
+    tiles_ref[...] = sum(in_ref[d, 64:72, :].astype(F32) for d in range(16))
+
+
+def turn_kernel(in_ref, out_ref, f_ref):
+    zq = lax.axis_index("zq")
+    both = in_ref[zq].astype(F32) + in_ref[lax.rem(zq + 2, ZQ)].astype(F32)
+    f_ref[...] = both.reshape(f_ref.shape)
+    for zh in range(ZH):
+        rows = [f_ref[pl.ds(zh * 16 + k, Y, stride=32), :] for k in range(16)]
+        block = jnp.concatenate(rows, axis=0).astype(BF)
+        for q in range(ZQ):
+            out_ref[zh * ZQ + q] = block
+
+
+def correlate_kernel(in_ref, tiles_ref, out_ref, f_ref, a_ref, c_ref, d_ref):
     f_ref[...] = in_ref[...].astype(F32).reshape(f_ref.shape)
-    for zh in range(ZH):
-        for f in range(FRAMES):
-            rows = f_ref[pl.ds(zh * FRAMES + f, X * Y, stride=16), :].astype(BF)
-            for zq in range(ZQ):
-                out_ref[zh * ZQ + zq, f * X * Y : (f + 1) * X * Y, :] = rows
-    tiles_ref[...] = f_ref[pl.ds(14, X, stride=16 * Y), :]
-
-
-def correlate_kernel(in_ref, tiles_ref, out_ref, f_ref, a_ref, c_ref, d_ref):
-    def part(zh, zq, f):
-        return in_ref[zh * ZQ + zq, f * 32 : (f + 1) * 32, :].astype(F32)
-
-    for zh in range(ZH):
-        for zq in range(ZQ):
-            for f in range(4):
-                rows = part(zh, zq, f)
-                if f + 4 < FRAMES:
-                    if zq:
-                        rows = rows + part(zh, zq - 1, f + 4)
-                    else:
-                        spill = part(zh, ZQ - 1, f + 4)
-                        rows = rows + jnp.concatenate([jnp.zeros((Y, LANES), F32), spill[: 32 - Y]], axis=0)
-                f_ref[((zh * ZQ + zq) * 4 + f) * 32 : ((zh * ZQ + zq) * 4 + f + 1) * 32, :] = rows
     for zh in range(ZH):
         groups = [f_ref[pl.ds(zh * 384 + y, TIME, stride=Y), :] for y in range(Y)]
         for k, rows in enumerate(swap_chunks(groups, 16)):
@@ -169,19 +167,8 @@
                 at = block * 256 + s * 16
                 d_ref[at : at + 16, ch * LANES : (ch + 1) * LANES] = part.astype(BF)
 
-    lane = lax.broadcasted_iota(jnp.int32, (8, LANES), 1)
-    firsts, seconds = [], []
-    for half in range(2):
-        for shift, found in ((0, firsts), (64, seconds)):
-            total = None
-            for x in range(2):
-                rows = jnp.broadcast_to(tiles_ref[half * 2 + x : half * 2 + x + 1, :], (8, LANES))
-                rows = pltpu.roll(rows, shift, 1) if shift else rows
-                rows = jnp.where(lane < 4 * SLOT, rows, 0.0)
-                total = rows if total is None else total + pltpu.roll(rows, x * 4 * SLOT, 1)
-            found.append(total[0:1])
-    r = jnp.concatenate(firsts, axis=1).astype(jnp.int32)
-    s = jnp.concatenate(seconds, axis=1).astype(jnp.int32)
+    r = jnp.concatenate([tiles_ref[0:1], tiles_ref[1:2]], axis=1).astype(jnp.int32)
+    s = jnp.concatenate([tiles_ref[2:3], tiles_ref[3:4]], axis=1).astype(jnp.int32)
     rh, sh = jnp.where(r >= 16, 1, 0), jnp.where(s >= 16, 1, 0)
     index = (rh + sh) * 256 + (s - 16 * sh) * 16 + (r - 16 * rh)
     pick = jnp.where(lax.broadcasted_iota(jnp.int32, (768, 256), 0) == index, 1.0, 0.0).astype(BF)
@@ -209,7 +196,7 @@
     arrays = (tile_map.T, voltages, fir_taps, jnp.asarray(dft_table()))
     sent = pl.pallas_call(
         tap_kernel,
-        out_shape=jax.ShapeDtypeStruct((ZR * C, 264, LANES), BF),
+        out_shape=jax.ShapeDtypeStruct((X * ZR * C, 72, LANES), BF),
         in_specs=[hbm] * 4,
         scratch_shapes=[
             pltpu.SMEM((2, OWN), jnp.int32),
@@ -221,25 +208,25 @@
         compiler_params=PARAMS,
         name="taps",
     )(*(pltpu.with_memory_space_constraint(a, pltpu.MemorySpace.HBM) for a in arrays))
-    came = lax.all_to_all(sent, ("zr", "c"), 0, 0, tiled=True)
-    sent = pl.pallas_call(
+    came = lax.all_to_all(sent, ("x", "zr", "c"), 0, 0, tiled=True)
+    sent, tiles = pl.pallas_call(
         sum_kernel,
-        out_shape=jax.ShapeDtypeStruct((X * Y, 16, LANES), BF),
-        scratch_shapes=[pltpu.VMEM((X * Y * 16, LANES), F32)],
+        out_shape=(
+            jax.ShapeDtypeStruct((ZQ, Y, 32, LANES), BF),
+            jax.ShapeDtypeStruct((8, LANES), F32),
+        ),
+        scratch_shapes=[pltpu.VMEM((512, LANES), F32)],
         compiler_params=PARAMS,
         name="sum",
     )(came)
-    came = lax.all_to_all(sent, ("x", "y"), 0, 0, tiled=True)
-    sent, tiles = pl.pallas_call(
+    came = lax.all_to_all(sent.reshape(ZQ * Y, 32, LANES), ("zq", "y"), 0, 0, tiled=True)
+    sent = pl.pallas_call(
         turn_kernel,
-        out_shape=(
-            jax.ShapeDtypeStruct((ZH * ZQ, FRAMES * X * Y, LANES), BF),
-            jax.ShapeDtypeStruct((X, LANES), F32),
-        ),
-        scratch_shapes=[pltpu.VMEM((X * Y * 16, LANES), F32)],
+        out_shape=jax.ShapeDtypeStruct((ZH * ZQ, 128, LANES), BF),
+        scratch_shapes=[pltpu.VMEM((256, LANES), F32)],
         compiler_params=PARAMS,
         name="turn",
-    )(came)
+    )(came.reshape(ZQ, Y, 32, LANES))
     came = lax.all_to_all(sent, ("zh", "zq"), 0, 0, tiled=True)
     sent = pl.pallas_call(
         correlate_kernel,

time: 76.3 us -> 82.4 us (1.080)
  blocking collectives: 70.2 us -> 76.5 us
    all_to_all x1 -> x2, blocking collectives: 12.5 us -> 35 us  [per_device(): came = lax.all_to_all(sent, ('x', 'zr', 'c'), 0, 0, tiled=True)]
    all_to_all x1, blocking collectives: 27 us -> 18.7 us  [per_device(): came = lax.all_to_all(sent, ('zh', 'zq'), 0, 0, tiled=True)]
    all_to_all x2 -> x1, blocking collectives: 30.7 us -> 22.8 us  [per_device(): lax.all_to_all(sent.reshape(ZQ * Y, 32, LANES), ('zq', 'y'), 0, 0, tiled=...]
where the time goes in v4:
time: 82.4 us; the launch traced here: 82.1 us
  blocking collectives  76.5 us (93%)
  Pallas kernels  5.62 us (7%)
    all_to_all x2, blocking collectives, per_device(): came = lax.all_to_all(sent, ('x', 'zr', 'c'), 0, 0, tiled=True)  35 us
    all_to_all x1, blocking collectives, per_device(): lax.all_to_all(sent.reshape(ZQ * Y, 32, LANES), ('zq', 'y'), 0, 0, tiled=...  22.8 us
    all_to_all x1, blocking collectives, per_device(): came = lax.all_to_all(sent, ('zh', 'zq'), 0, 0, tiled=True)  18.7 us
    pallas_call x1, Pallas kernels, per_device(): pl.pallas_call(correlate_kernel, out_shape=jax.ShapeDtypeStruct((16, 4 *...  2.29 us
    pallas_call x1, Pallas kernels, per_device(): pl.pallas_call(tap_kernel, out_shape=jax.ShapeDtypeStruct((X * ZR * C, 72...  2.26 us

profile of v4, /device:TPU:1, one launch (start us, length us, event | category | flops | bytes accessed | tf_op | source)
XLA Modules:
  0.0 82.1 jit_solution(17169592427017140493)
XLA Ops:
  0.0 2.3 %taps.1 = bf16[16,72,128]{2,1,0:T(8,128)(2,1)S(1)} custom-call(s32[2,11]{1,0:T(2,128)} %bitcast.5, s32[1,16,2048]{2,1,0:T(8,128)} %volts_hbm.1, f32[4,1024]{1,0:T(4,128)} %fir_hbm.1, bf16[256,2048]{1,0:T(8,128)(2,1)} %constant.2.clone.table_hbm), custom_call_target="tpu_custom_call" | custom-call | tf_op jit(solution)/shard_map/taps/pallas_call | solution.py:197
  2.3 20.4 %all_to_all.20.in_ref = bf16[16,72,128]{2,1,0:T(8,128)(2,1)S(1)} all-to-all(bf16[16,72,128]{2,1,0:T(8,128)(2,1)S(1)} %taps.1), channel_id=1, replica_groups=mesh['zh'=2,'y'=8,'x'=4,'zq'=3,'zr'=2,'c'=2] {'x','zr','c'}, dimensions={0} | all-to-all | bytes 589824 | tf_op jit(solution)/shard_map/all_to_all | solution.py:211
  22.6 0.2 sum.1
  22.8 22.8 %all_to_all.21 = bf16[24,32,128]{2,1,0:T(8,128)(2,1)S(1)} all-to-all(bf16[24,32,128]{2,1,0:T(8,128)(2,1)S(1)} %bitcast.4), channel_id=1, replica_groups=mesh['zh'=2,'y'=8,'x'=4,'zq'=3,'zr'=2,'c'=2] {'zq','y'}, dimensions={0} | all-to-all | bytes 393216 | tf_op jit(solution)/shard_map/all_to_all | solution.py:222
  45.6 0.1 turn.1
  45.7 18.7 %all_to_all.22.in_ref = bf16[6,128,128]{2,1,0:T(8,128)(2,1)S(1)} all-to-all(bf16[6,128,128]{2,1,0:T(8,128)(2,1)S(1)} %turn.1), channel_id=1, replica_groups=mesh['zh'=2,'y'=8,'x'=4,'zq'=3,'zr'=2,'c'=2] {'zh','zq'}, dimensions={0} | all-to-all | bytes 393216 | tf_op jit(solution)/shard_map/all_to_all | solution.py:230
  64.4 2.3 %correlate.1 = bf16[16,48,128]{2,1,0:T(8,128)(2,1)S(1)} custom-call(bf16[6,128,128]{2,1,0:T(8,128)(2,1)S(1)} %all_to_all.22.in_ref, f32[8,128]{1,0:T(8,128)S(1)} %get-tuple-element.8.tiles_ref), custom_call_target="tpu_custom_call" | custom-call | tf_op jit(solution)/shard_map/correlate/pallas_call | solution.py:231
  66.7 14.6 %all_to_all.23.in_ref = bf16[16,48,128]{2,1,0:T(8,128)(2,1)S(1)} all-to-all(bf16[16,48,128]{2,1,0:T(8,128)(2,1)S(1)} %correlate.1), channel_id=1, replica_groups=mesh['zh'=2,'y'=8,'x'=4,'zq'=3,'zr'=2,'c'=2] {'x','zr','c'}, dimensions={0} | all-to-all | bytes 393216 | tf_op jit(solution)/shard_map/all_to_all | solution.py:243
  81.3 0.8 place.1

commit v5 on v4

--- a/solution.py
+++ b/solution.py
@@ -108,44 +108,44 @@
 
 
 def sum_kernel(in_ref, out_ref, tiles_ref, f_ref):
-    zq = lax.axis_index("zq")
-    sums = [[None] * (FRAMES + 1) for _ in range(X)]
     for x in range(X):
         for f in range(FRAMES):
+            total = None
             for k in range(TAPS):
                 if 0 <= f - k < 4:
                     part = in_ref[x * 4 + f - k, k * 16 : (k + 1) * 16, :].astype(F32)
-                    sums[x][f] = part if sums[x][f] is None else sums[x][f] + part
-        sums[x][FRAMES] = jnp.zeros((16, LANES), F32)
-    zeros = jnp.zeros((16, LANES), F32)
-    for spill in range(2):
-        for x in range(X):
+                    total = part if total is None else total + part
+            for zh in range(ZH):
+                f_ref[pl.ds((zh * X + x) * FRAMES + f, Y, stride=56), :] = total[zh * Y : (zh + 1) * Y]
+    out_ref[...] = f_ref[...].reshape(Y, 56, LANES).astype(BF)
+    tiles_ref[...] = sum(in_ref[d, 64:72, :].astype(F32) for d in range(16))
+
+
+def turn_kernel(in_ref, out_ref, f_ref):
+    f_ref[...] = in_ref[...].astype(F32).reshape(f_ref.shape)
+    for zh in range(ZH):
+        for f in range(FRAMES):
+            rows = [f_ref[pl.ds((zh * X + x) * FRAMES + f, Y, stride=56), :] for x in range(X)]
+            block = jnp.concatenate(rows, axis=0).astype(BF)
+            for zq in range(ZQ):
+                out_ref[zh * ZQ + zq, f * 32 : (f + 1) * 32, :] = block
+
+
+def correlate_kernel(in_ref, tiles_ref, out_ref, f_ref, a_ref, c_ref, d_ref):
+    def part(zh, zq, f):
+        return in_ref[zh * ZQ + zq, f * 32 : (f + 1) * 32, :].astype(F32)
+
+    for zh in range(ZH):
+        for zq in range(ZQ):
             for f in range(4):
-                rows = sums[x][4 * spill + f]
-                if spill:
-                    rows = jnp.where(zq == ZQ - 1, sums[x - 1][4 + f] if x else zeros, rows)
-                for zh in range(ZH):
-                    at = spill * 256 + zh * 16 + x * 4 + f
-                    f_ref[pl.ds(at, Y, stride=32), :] = rows[zh * Y : (zh + 1) * Y]
-    out_ref[zq] = f_ref[:256, :].reshape(Y, 32, LANES).astype(BF)
-    out_ref[lax.rem(zq + 1, ZQ)] = f_ref[256:, :].reshape(Y, 32, LANES).astype(BF)
-    out_ref[lax.rem(zq + 2, ZQ)] = jnp.zeros((Y, 32, LANES), BF)
-    tiles_ref[...] = sum(in_ref[d, 64:72, :].astype(F32) for d in range(16))
-
-
-def turn_kernel(in_ref, out_ref, f_ref):
-    zq = lax.axis_index("zq")
-    both = in_ref[zq].astype(F32) + in_ref[lax.rem(zq + 2, ZQ)].astype(F32)
-    f_ref[...] = both.reshape(f_ref.shape)
-    for zh in range(ZH):
-        rows = [f_ref[pl.ds(zh * 16 + k, Y, stride=32), :] for k in range(16)]
-        block = jnp.concatenate(rows, axis=0).astype(BF)
-        for q in range(ZQ):
-            out_ref[zh * ZQ + q] = block
-
-
-def correlate_kernel(in_ref, tiles_ref, out_ref, f_ref, a_ref, c_ref, d_ref):
-    f_ref[...] = in_ref[...].astype(F32).reshape(f_ref.shape)
+                rows = part(zh, zq, f)
+                if f + 4 < FRAMES:
+                    if zq:
+                        rows = rows + part(zh, zq - 1, f + 4)
+                    else:
+                        spill = part(zh, ZQ - 1, f + 4)
+                        rows = rows + jnp.concatenate([jnp.zeros((Y, LANES), F32), spill[: 32 - Y]], axis=0)
+                f_ref[((zh * ZQ + zq) * 4 + f) * 32 : ((zh * ZQ + zq) * 4 + f + 1) * 32, :] = rows
     for zh in range(ZH):
         groups = [f_ref[pl.ds(zh * 384 + y, TIME, stride=Y), :] for y in range(Y)]
         for k, rows in enumerate(swap_chunks(groups, 16)):
@@ -212,21 +212,21 @@
     sent, tiles = pl.pallas_call(
         sum_kernel,
         out_shape=(
-            jax.ShapeDtypeStruct((ZQ, Y, 32, LANES), BF),
+            jax.ShapeDtypeStruct((Y, 56, LANES), BF),
             jax.ShapeDtypeStruct((8, LANES), F32),
         ),
-        scratch_shapes=[pltpu.VMEM((512, LANES), F32)],
+        scratch_shapes=[pltpu.VMEM((Y * 56, LANES), F32)],
         compiler_params=PARAMS,
         name="sum",
     )(came)
-    came = lax.all_to_all(sent.reshape(ZQ * Y, 32, LANES), ("zq", "y"), 0, 0, tiled=True)
+    came = lax.all_to_all(sent, "y", 0, 0, tiled=True)
     sent = pl.pallas_call(
         turn_kernel,
-        out_shape=jax.ShapeDtypeStruct((ZH * ZQ, 128, LANES), BF),
-        scratch_shapes=[pltpu.VMEM((256, LANES), F32)],
+        out_shape=jax.ShapeDtypeStruct((ZH * ZQ, FRAMES * X * Y, LANES), BF),
+        scratch_shapes=[pltpu.VMEM((Y * 56, LANES), F32)],
         compiler_params=PARAMS,
         name="turn",
-    )(came.reshape(ZQ, Y, 32, LANES))
+    )(came)
     came = lax.all_to_all(sent, ("zh", "zq"), 0, 0, tiled=True)
     sent = pl.pallas_call(
         correlate_kernel,

time: 82.4 us -> 76.8 us (0.932)
  blocking collectives: 76.5 us -> 71.1 us
    all_to_all x1, blocking collectives: 22.8 us -> 10.2 us  [per_device(): came = lax.all_to_all(sent, 'y', 0, 0, tiled=True)]
    all_to_all x1, blocking collectives: 18.7 us -> 26.9 us  [per_device(): came = lax.all_to_all(sent, ('zh', 'zq'), 0, 0, tiled=True)]
    all_to_all x2, blocking collectives: 35 us -> 33.9 us  [per_device(): came = lax.all_to_all(sent, ('x', 'zr', 'c'), 0, 0, tiled=True)]
where the time goes in v5:
time: 76.8 us; the launch traced here: 76.5 us
  blocking collectives  71.1 us (93%)
  Pallas kernels  5.46 us (7%)
    all_to_all x2, blocking collectives, per_device(): came = lax.all_to_all(sent, ('x', 'zr', 'c'), 0, 0, tiled=True)  33.9 us
    all_to_all x1, blocking collectives, per_device(): came = lax.all_to_all(sent, ('zh', 'zq'), 0, 0, tiled=True)  26.9 us
    all_to_all x1, blocking collectives, per_device(): came = lax.all_to_all(sent, 'y', 0, 0, tiled=True)  10.2 us
    pallas_call x1, Pallas kernels, per_device(): pl.pallas_call(correlate_kernel, out_shape=jax.ShapeDtypeStruct((16, 4 *...  2.29 us
    pallas_call x1, Pallas kernels, per_device(): pl.pallas_call(tap_kernel, out_shape=jax.ShapeDtypeStruct((X * ZR * C, 72...  2.26 us

profile of v5, /device:TPU:1, one launch (start us, length us, event | category | flops | bytes accessed | tf_op | source)
XLA Modules:
  0.0 76.5 jit_solution(5302243458351286111)
XLA Ops:
  0.0 2.3 %taps.1 = bf16[16,72,128]{2,1,0:T(8,128)(2,1)S(1)} custom-call(s32[2,11]{1,0:T(2,128)} %bitcast.1, s32[1,16,2048]{2,1,0:T(8,128)} %volts_hbm.1, f32[4,1024]{1,0:T(4,128)} %fir_hbm.1, bf16[256,2048]{1,0:T(8,128)(2,1)} %constant.2.clone.table_hbm), custom_call_target="tpu_custom_call" | custom-call | tf_op jit(solution)/shard_map/taps/pallas_call | solution.py:197
  2.3 20.4 %all_to_all.20.in_ref = bf16[16,72,128]{2,1,0:T(8,128)(2,1)S(1)} all-to-all(bf16[16,72,128]{2,1,0:T(8,128)(2,1)S(1)} %taps.1), channel_id=1, replica_groups=mesh['zh'=2,'y'=8,'x'=4,'zq'=3,'zr'=2,'c'=2] {'x','zr','c'}, dimensions={0} | all-to-all | bytes 589824 | tf_op jit(solution)/shard_map/all_to_all | solution.py:211
  22.6 0.1 sum.1
  22.7 10.2 %all_to_all.21.in_ref = bf16[8,56,128]{2,1,0:T(8,128)(2,1)S(1)} all-to-all(bf16[8,56,128]{2,1,0:T(8,128)(2,1)S(1)} %get-tuple-element.7), channel_id=1, replica_groups=mesh['zh'=2,'y'=8,'x'=4,'zq'=3,'zr'=2,'c'=2] {'y'}, dimensions={0} | all-to-all | bytes 229376 | tf_op jit(solution)/shard_map/all_to_all | solution.py:222
  32.9 0.1 turn.1
  33.0 26.9 %all_to_all.22.in_ref = bf16[6,224,128]{2,1,0:T(8,128)(2,1)S(1)} all-to-all(bf16[6,224,128]{2,1,0:T(8,128)(2,1)S(1)} %turn.1), channel_id=1, replica_groups=mesh['zh'=2,'y'=8,'x'=4,'zq'=3,'zr'=2,'c'=2] {'zh','zq'}, dimensions={0} | all-to-all | bytes 688128 | tf_op jit(solution)/shard_map/all_to_all | solution.py:230
  59.9 2.3 %correlate.1 = bf16[16,48,128]{2,1,0:T(8,128)(2,1)S(1)} custom-call(bf16[6,224,128]{2,1,0:T(8,128)(2,1)S(1)} %all_to_all.22.in_ref, f32[8,128]{1,0:T(8,128)S(1)} %get-tuple-element.8.tiles_ref), custom_call_target="tpu_custom_call" | custom-call | tf_op jit(solution)/shard_map/correlate/pallas_call | solution.py:231
  62.2 13.5 %all_to_all.23.in_ref = bf16[16,48,128]{2,1,0:T(8,128)(2,1)S(1)} all-to-all(bf16[16,48,128]{2,1,0:T(8,128)(2,1)S(1)} %correlate.1), channel_id=1, replica_groups=mesh['zh'=2,'y'=8,'x'=4,'zq'=3,'zr'=2,'c'=2] {'x','zr','c'}, dimensions={0} | all-to-all | bytes 393216 | tf_op jit(solution)/shard_map/all_to_all | solution.py:243
  75.7 0.8 %place.1 = f32[11,64,128]{2,1,0:T(8,128)} custom-call(bf16[16,48,128]{2,1,0:T(8,128)(2,1)S(1)} %all_to_all.23.in_ref), custom_call_target="tpu_custom_call" | custom-call | tf_op jit(solution)/shard_map/place/pallas_call | solution.py:244

commit v6 on v5

--- a/solution.py
+++ b/solution.py
@@ -150,7 +150,9 @@
         groups = [f_ref[pl.ds(zh * 384 + y, TIME, stride=Y), :] for y in range(Y)]
         for k, rows in enumerate(swap_chunks(groups, 16)):
             ch, p = divmod(k, 2)
-            a_ref[ch, p * TIME : (p + 1) * TIME, zh * LANES : (zh + 1) * LANES] = rows.astype(BF)
+            for h, half in enumerate(split(rows)):
+                at = (2 * h + p) * TIME
+                a_ref[ch, at : at + TIME, zh * LANES : (zh + 1) * LANES] = half
 
     i = lax.broadcasted_iota(jnp.int32, (256, 256), 0)
     j = lax.broadcasted_iota(jnp.int32, (256, 256), 1)
@@ -158,9 +160,15 @@
     for ch in range(4):
         cols = a_ref[ch]
         left = dot(cols, order, (1, 0))
-        re, im = left[:TIME], left[TIME:]
-        both = jnp.concatenate([jnp.concatenate([re, im], axis=0), jnp.concatenate([im, -re], axis=0)], axis=1)
-        c_ref[...] = dot(both.astype(BF), cols, (0, 0)) * (1.0 / TIME)
+        parts = []
+        for h in range(2):
+            re, im = left[2 * h * TIME : (2 * h + 1) * TIME], left[(2 * h + 1) * TIME : (2 * h + 2) * TIME]
+            real, imag = jnp.concatenate([re, im], axis=0), jnp.concatenate([im, -re], axis=0)
+            parts.append(jnp.concatenate([real, imag], axis=1).astype(BF))
+        high, low = parts
+        total = dot(jnp.concatenate([high, low], axis=0), jnp.concatenate([cols[: 2 * TIME]] * 2, axis=0), (0, 0))
+        total = total + dot(high, cols[2 * TIME :], (0, 0))
+        c_ref[...] = total * (1.0 / TIME)
         for block, (h, g) in enumerate(((0, 0), (1, 0), (1, 1))):
             rows = [c_ref[k * 32 + g * 16 : k * 32 + g * 16 + 16, h * LANES : (h + 1) * LANES] for k in range(16)]
             for s, part in enumerate(swap_chunks(rows, 8)):
@@ -233,7 +241,7 @@
         out_shape=jax.ShapeDtypeStruct((16, 4 * SLOT, LANES), BF),
         scratch_shapes=[
             pltpu.VMEM((768, LANES), F32),
-            pltpu.VMEM((4, 2 * TIME, 256), BF),
+            pltpu.VMEM((4, 4 * TIME, 256), BF),
             pltpu.VMEM((512, 256), F32),
             pltpu.VMEM((768, 512), BF),
         ],

time: 76.8 us -> 77.8 us (1.013)
  Pallas kernels: 5.46 us -> 6.42 us
    pallas_call x1, Pallas kernels: 2.29 us -> 3.24 us  [per_device(): pl.pallas_call(correlate_kernel, out_shape=jax.ShapeDtypeStruct((16, 4 *...]
where the time goes in v6:
time: 77.8 us; the launch traced here: 77.5 us
  blocking collectives  71 us (91%)
  Pallas kernels  6.42 us (8%)
    all_to_all x2, blocking collectives, per_device(): came = lax.all_to_all(sent, ('x', 'zr', 'c'), 0, 0, tiled=True)  33.9 us
    all_to_all x1, blocking collectives, per_device(): came = lax.all_to_all(sent, ('zh', 'zq'), 0, 0, tiled=True)  26.9 us
    all_to_all x1, blocking collectives, per_device(): came = lax.all_to_all(sent, 'y', 0, 0, tiled=True)  10.2 us
    pallas_call x1, Pallas kernels, per_device(): pl.pallas_call(correlate_kernel, out_shape=jax.ShapeDtypeStruct((16, 4 *...  3.24 us
    pallas_call x1, Pallas kernels, per_device(): pl.pallas_call(tap_kernel, out_shape=jax.ShapeDtypeStruct((X * ZR * C, 72...  2.26 us

profile of v6, /device:TPU:1, one launch (start us, length us, event | category | flops | bytes accessed | tf_op | source)
XLA Modules:
  0.0 77.5 jit_solution(2774495035735231921)
XLA Ops:
  0.0 2.3 %taps.1 = bf16[16,72,128]{2,1,0:T(8,128)(2,1)S(1)} custom-call(s32[2,11]{1,0:T(2,128)} %bitcast.1, s32[1,16,2048]{2,1,0:T(8,128)} %volts_hbm.1, f32[4,1024]{1,0:T(4,128)} %fir_hbm.1, bf16[256,2048]{1,0:T(8,128)(2,1)} %constant.2.clone.table_hbm), custom_call_target="tpu_custom_call" | custom-call | tf_op jit(solution)/shard_map/taps/pallas_call | solution.py:205
  2.3 20.4 %all_to_all.20.in_ref = bf16[16,72,128]{2,1,0:T(8,128)(2,1)S(1)} all-to-all(bf16[16,72,128]{2,1,0:T(8,128)(2,1)S(1)} %taps.1), channel_id=1, replica_groups=mesh['zh'=2,'y'=8,'x'=4,'zq'=3,'zr'=2,'c'=2] {'x','zr','c'}, dimensions={0} | all-to-all | bytes 589824 | tf_op jit(solution)/shard_map/all_to_all | solution.py:219
  22.6 0.1 sum.1
  22.7 10.2 %all_to_all.21.in_ref = bf16[8,56,128]{2,1,0:T(8,128)(2,1)S(1)} all-to-all(bf16[8,56,128]{2,1,0:T(8,128)(2,1)S(1)} %get-tuple-element.7), channel_id=1, replica_groups=mesh['zh'=2,'y'=8,'x'=4,'zq'=3,'zr'=2,'c'=2] {'y'}, dimensions={0} | all-to-all | bytes 229376 | tf_op jit(solution)/shard_map/all_to_all | solution.py:230
  32.9 0.1 turn.1
  33.0 26.9 %all_to_all.22.in_ref = bf16[6,224,128]{2,1,0:T(8,128)(2,1)S(1)} all-to-all(bf16[6,224,128]{2,1,0:T(8,128)(2,1)S(1)} %turn.1), channel_id=1, replica_groups=mesh['zh'=2,'y'=8,'x'=4,'zq'=3,'zr'=2,'c'=2] {'zh','zq'}, dimensions={0} | all-to-all | bytes 688128 | tf_op jit(solution)/shard_map/all_to_all | solution.py:238
  59.9 3.2 %correlate.1 = bf16[16,48,128]{2,1,0:T(8,128)(2,1)S(1)} custom-call(bf16[6,224,128]{2,1,0:T(8,128)(2,1)S(1)} %all_to_all.22.in_ref, f32[8,128]{1,0:T(8,128)S(1)} %get-tuple-element.8.tiles_ref), custom_call_target="tpu_custom_call" | custom-call | tf_op jit(solution)/shard_map/correlate/pallas_call | solution.py:239
  63.1 13.5 %all_to_all.23.in_ref = bf16[16,48,128]{2,1,0:T(8,128)(2,1)S(1)} all-to-all(bf16[16,48,128]{2,1,0:T(8,128)(2,1)S(1)} %correlate.1), channel_id=1, replica_groups=mesh['zh'=2,'y'=8,'x'=4,'zq'=3,'zr'=2,'c'=2] {'x','zr','c'}, dimensions={0} | all-to-all | bytes 393216 | tf_op jit(solution)/shard_map/all_to_all | solution.py:251
  76.7 0.8 %place.1 = f32[11,64,128]{2,1,0:T(8,128)} custom-call(bf16[16,48,128]{2,1,0:T(8,128)(2,1)S(1)} %all_to_all.23.in_ref), custom_call_target="tpu_custom_call" | custom-call | tf_op jit(solution)/shard_map/place/pallas_call | solution.py:252

commit v7 on v5

--- a/solution.py
+++ b/solution.py
@@ -115,39 +115,31 @@
                 if 0 <= f - k < 4:
                     part = in_ref[x * 4 + f - k, k * 16 : (k + 1) * 16, :].astype(F32)
                     total = part if total is None else total + part
-            for zh in range(ZH):
-                f_ref[pl.ds((zh * X + x) * FRAMES + f, Y, stride=56), :] = total[zh * Y : (zh + 1) * Y]
-    out_ref[...] = f_ref[...].reshape(Y, 56, LANES).astype(BF)
+            f_ref[pl.ds(x * 8 + f, ZH * Y, stride=32), :] = total
+        f_ref[pl.ds(x * 8 + FRAMES, ZH * Y, stride=32), :] = jnp.zeros((ZH * Y, LANES), F32)
+    for zh in range(ZH):
+        block = f_ref[zh * 256 : (zh + 1) * 256, :].reshape(Y, 32, LANES).astype(BF)
+        for zq in range(ZQ):
+            at = (zh * ZQ + zq) * Y
+            out_ref[at : at + Y] = block
     tiles_ref[...] = sum(in_ref[d, 64:72, :].astype(F32) for d in range(16))
 
 
-def turn_kernel(in_ref, out_ref, f_ref):
+def correlate_kernel(in_ref, tiles_ref, out_ref, f_ref, a_ref, c_ref, d_ref):
     f_ref[...] = in_ref[...].astype(F32).reshape(f_ref.shape)
+    upper = lax.broadcasted_iota(jnp.int32, (8, LANES), 0) < 4
+
+    def frames(zh, y):
+        at = [((zh * ZQ + q % ZQ) * Y + y) * 32 + q // ZQ * 8 for q in range(X * ZQ)]
+        own = [f_ref[a : a + 8, :] for a in at]
+        turned = [pltpu.roll(v, 4, 0) for v in own]
+        before = [jnp.zeros((8, LANES), F32)] + turned
+        return jnp.concatenate(
+            [own[q] + jnp.where(upper, before[q], turned[q + 1]) for q in range(0, X * ZQ, 2)], axis=0
+        )
+
     for zh in range(ZH):
-        for f in range(FRAMES):
-            rows = [f_ref[pl.ds((zh * X + x) * FRAMES + f, Y, stride=56), :] for x in range(X)]
-            block = jnp.concatenate(rows, axis=0).astype(BF)
-            for zq in range(ZQ):
-                out_ref[zh * ZQ + zq, f * 32 : (f + 1) * 32, :] = block
-
-
-def correlate_kernel(in_ref, tiles_ref, out_ref, f_ref, a_ref, c_ref, d_ref):
-    def part(zh, zq, f):
-        return in_ref[zh * ZQ + zq, f * 32 : (f + 1) * 32, :].astype(F32)
-
-    for zh in range(ZH):
-        for zq in range(ZQ):
-            for f in range(4):
-                rows = part(zh, zq, f)
-                if f + 4 < FRAMES:
-                    if zq:
-                        rows = rows + part(zh, zq - 1, f + 4)
-                    else:
-                        spill = part(zh, ZQ - 1, f + 4)
-                        rows = rows + jnp.concatenate([jnp.zeros((Y, LANES), F32), spill[: 32 - Y]], axis=0)
-                f_ref[((zh * ZQ + zq) * 4 + f) * 32 : ((zh * ZQ + zq) * 4 + f + 1) * 32, :] = rows
-    for zh in range(ZH):
-        groups = [f_ref[pl.ds(zh * 384 + y, TIME, stride=Y), :] for y in range(Y)]
+        groups = [frames(zh, y) for y in range(Y)]
         for k, rows in enumerate(swap_chunks(groups, 16)):
             ch, p = divmod(k, 2)
             a_ref[ch, p * TIME : (p + 1) * TIME, zh * LANES : (zh + 1) * LANES] = rows.astype(BF)
@@ -179,7 +171,7 @@
             at = (ch // 2) * 256 + (d // 8) * LANES + (d % 8) * SLOT
             rows = c_ref[at : at + SLOT, (ch % 2) * LANES : (ch % 2 + 1) * LANES]
             f_ref[d * 48 + ch * SLOT : d * 48 + (ch + 1) * SLOT, :] = rows
-    out_ref[...] = f_ref[...].reshape(16, 48, LANES).astype(BF)
+    out_ref[...] = f_ref[: 16 * 48, :].reshape(16, 48, LANES).astype(BF)
 
 
 def place_kernel(in_ref, out_ref, f_ref):
@@ -212,27 +204,19 @@
     sent, tiles = pl.pallas_call(
         sum_kernel,
         out_shape=(
-            jax.ShapeDtypeStruct((Y, 56, LANES), BF),
+            jax.ShapeDtypeStruct((ZH * ZQ * Y, 32, LANES), BF),
             jax.ShapeDtypeStruct((8, LANES), F32),
         ),
-        scratch_shapes=[pltpu.VMEM((Y * 56, LANES), F32)],
+        scratch_shapes=[pltpu.VMEM((ZH * Y * 32, LANES), F32)],
         compiler_params=PARAMS,
         name="sum",
     )(came)
-    came = lax.all_to_all(sent, "y", 0, 0, tiled=True)
-    sent = pl.pallas_call(
-        turn_kernel,
-        out_shape=jax.ShapeDtypeStruct((ZH * ZQ, FRAMES * X * Y, LANES), BF),
-        scratch_shapes=[pltpu.VMEM((Y * 56, LANES), F32)],
-        compiler_params=PARAMS,
-        name="turn",
-    )(came)
-    came = lax.all_to_all(sent, ("zh", "zq"), 0, 0, tiled=True)
+    came = lax.all_to_all(sent, ("zh", "zq", "y"), 0, 0, tiled=True)
     sent = pl.pallas_call(
         correlate_kernel,
         out_shape=jax.ShapeDtypeStruct((16, 4 * SLOT, LANES), BF),
         scratch_shapes=[
-            pltpu.VMEM((768, LANES), F32),
+            pltpu.VMEM((ZH * ZQ * Y * 32, LANES), F32),
             pltpu.VMEM((4, 2 * TIME, 256), BF),
             pltpu.VMEM((512, 256), F32),
             pltpu.VMEM((768, 512), BF),

time: 76.8 us -> 74.5 us (0.970)
  blocking collectives: 71.1 us -> 68.8 us
    all_to_all x2 -> x1, blocking collectives: 37.1 us -> 34.9 us  [per_device(): came = lax.all_to_all(sent, ('zh', 'zq', 'y'), 0, 0, tiled=True)]
where the time goes in v7:
time: 74.5 us; the launch traced here: 74.3 us
  blocking collectives  68.8 us (92%)
  Pallas kernels  5.54 us (7%)
    all_to_all x1, blocking collectives, per_device(): came = lax.all_to_all(sent, ('zh', 'zq', 'y'), 0, 0, tiled=True)  34.9 us
    all_to_all x2, blocking collectives, per_device(): came = lax.all_to_all(sent, ('x', 'zr', 'c'), 0, 0, tiled=True)  33.9 us
    pallas_call x1, Pallas kernels, per_device(): pl.pallas_call(tap_kernel, out_shape=jax.ShapeDtypeStruct((X * ZR * C, 72...  2.26 us
    pallas_call x1, Pallas kernels, per_device(): pl.pallas_call(correlate_kernel, out_shape=jax.ShapeDtypeStruct((16, 4 *...  2.24 us

profile of v7, /device:TPU:1, one launch (start us, length us, event | category | flops | bytes accessed | tf_op | source)
XLA Modules:
  0.0 74.3 jit_solution(1024720020021012045)
XLA Ops:
  0.0 2.3 %taps.1 = bf16[16,72,128]{2,1,0:T(8,128)(2,1)S(1)} custom-call(s32[2,11]{1,0:T(2,128)} %bitcast.1, s32[1,16,2048]{2,1,0:T(8,128)} %volts_hbm.1, f32[4,1024]{1,0:T(4,128)} %fir_hbm.1, bf16[256,2048]{1,0:T(8,128)(2,1)} %constant.2.clone.table_hbm), custom_call_target="tpu_custom_call" | custom-call | tf_op jit(solution)/shard_map/taps/pallas_call | solution.py:189
  2.3 20.4 %all_to_all.15.in_ref = bf16[16,72,128]{2,1,0:T(8,128)(2,1)S(1)} all-to-all(bf16[16,72,128]{2,1,0:T(8,128)(2,1)S(1)} %taps.1), channel_id=1, replica_groups=mesh['zh'=2,'y'=8,'x'=4,'zq'=3,'zr'=2,'c'=2] {'x','zr','c'}, dimensions={0} | all-to-all | bytes 589824 | tf_op jit(solution)/shard_map/all_to_all | solution.py:203
  22.6 0.2 sum.1
  22.9 34.9 %all_to_all.16.in_ref = bf16[48,32,128]{2,1,0:T(8,128)(2,1)S(1)} all-to-all(bf16[48,32,128]{2,1,0:T(8,128)(2,1)S(1)} %get-tuple-element.7), channel_id=1, replica_groups=mesh['zh'=2,'y'=8,'x'=4,'zq'=3,'zr'=2,'c'=2] {'zh','zq','y'}, dimensions={0} | all-to-all | bytes 786432 | tf_op jit(solution)/shard_map/all_to_all | solution.py:214
  57.8 2.2 %correlate.1 = bf16[16,48,128]{2,1,0:T(8,128)(2,1)S(1)} custom-call(bf16[48,32,128]{2,1,0:T(8,128)(2,1)S(1)} %all_to_all.16.in_ref, f32[8,128]{1,0:T(8,128)S(1)} %get-tuple-element.8.tiles_ref), custom_call_target="tpu_custom_call" | custom-call | tf_op jit(solution)/shard_map/correlate/pallas_call | solution.py:215
  60.0 13.5 %all_to_all.17.in_ref = bf16[16,48,128]{2,1,0:T(8,128)(2,1)S(1)} all-to-all(bf16[16,48,128]{2,1,0:T(8,128)(2,1)S(1)} %correlate.1), channel_id=1, replica_groups=mesh['zh'=2,'y'=8,'x'=4,'zq'=3,'zr'=2,'c'=2] {'x','zr','c'}, dimensions={0} | all-to-all | bytes 393216 | tf_op jit(solution)/shard_map/all_to_all | solution.py:227
  73.5 0.8 %place.1 = f32[11,64,128]{2,1,0:T(8,128)} custom-call(bf16[16,48,128]{2,1,0:T(8,128)(2,1)S(1)} %all_to_all.17.in_ref), custom_call_target="tpu_custom_call" | custom-call | tf_op jit(solution)/shard_map/place/pallas_call | solution.py:228

commit v8 on v7

--- a/solution.py
+++ b/solution.py
@@ -120,8 +120,7 @@
     for zh in range(ZH):
         block = f_ref[zh * 256 : (zh + 1) * 256, :].reshape(Y, 32, LANES).astype(BF)
         for zq in range(ZQ):
-            at = (zh * ZQ + zq) * Y
-            out_ref[at : at + Y] = block
+            out_ref[:, zq * ZH + zh] = block
     tiles_ref[...] = sum(in_ref[d, 64:72, :].astype(F32) for d in range(16))
 
 
@@ -130,7 +129,7 @@
     upper = lax.broadcasted_iota(jnp.int32, (8, LANES), 0) < 4
 
     def frames(zh, y):
-        at = [((zh * ZQ + q % ZQ) * Y + y) * 32 + q // ZQ * 8 for q in range(X * ZQ)]
+        at = [((y * ZQ + q % ZQ) * ZH + zh) * 32 + q // ZQ * 8 for q in range(X * ZQ)]
         own = [f_ref[a : a + 8, :] for a in at]
         turned = [pltpu.roll(v, 4, 0) for v in own]
         before = [jnp.zeros((8, LANES), F32)] + turned
@@ -204,14 +203,14 @@
     sent, tiles = pl.pallas_call(
         sum_kernel,
         out_shape=(
-            jax.ShapeDtypeStruct((ZH * ZQ * Y, 32, LANES), BF),
+            jax.ShapeDtypeStruct((Y, ZQ * ZH, 32, LANES), BF),
             jax.ShapeDtypeStruct((8, LANES), F32),
         ),
         scratch_shapes=[pltpu.VMEM((ZH * Y * 32, LANES), F32)],
         compiler_params=PARAMS,
         name="sum",
     )(came)
-    came = lax.all_to_all(sent, ("zh", "zq", "y"), 0, 0, tiled=True)
+    came = lax.all_to_all(sent.reshape(Y * ZQ * ZH, 32, LANES), ("y", "zq", "zh"), 0, 0, tiled=True)
     sent = pl.pallas_call(
         correlate_kernel,
         out_shape=jax.ShapeDtypeStruct((16, 4 * SLOT, LANES), BF),

time: 74.5 us -> 73.7 us (0.989)
  blocking collectives: 68.8 us -> 67.8 us
    all_to_all x1, blocking collectives: 34.9 us -> 33.6 us  [per_device(): lax.all_to_all(sent.reshape(Y * ZQ * ZH, 32, LANES), ('y', 'zq', 'zh'), 0...]
where the time goes in v8:
time: 73.7 us; the launch traced here: 73.4 us
  blocking collectives  67.8 us (92%)
  Pallas kernels  5.55 us (8%)
    all_to_all x2, blocking collectives, per_device(): came = lax.all_to_all(sent, ('x', 'zr', 'c'), 0, 0, tiled=True)  34.3 us
    all_to_all x1, blocking collectives, per_device(): lax.all_to_all(sent.reshape(Y * ZQ * ZH, 32, LANES), ('y', 'zq', 'zh'), 0...  33.6 us
    pallas_call x1, Pallas kernels, per_device(): pl.pallas_call(tap_kernel, out_shape=jax.ShapeDtypeStruct((X * ZR * C, 72...  2.26 us
    pallas_call x1, Pallas kernels, per_device(): pl.pallas_call(correlate_kernel, out_shape=jax.ShapeDtypeStruct((16, 4 *...  2.25 us

profile of v8, /device:TPU:1, one launch (start us, length us, event | category | flops | bytes accessed | tf_op | source)
XLA Modules:
  0.0 73.4 jit_solution(6804971034098036456)
XLA Ops:
  0.0 2.3 %taps.1 = bf16[16,72,128]{2,1,0:T(8,128)(2,1)S(1)} custom-call(s32[2,11]{1,0:T(2,128)} %bitcast.3, s32[1,16,2048]{2,1,0:T(8,128)} %volts_hbm.1, f32[4,1024]{1,0:T(4,128)} %fir_hbm.1, bf16[256,2048]{1,0:T(8,128)(2,1)} %constant.2.clone.table_hbm), custom_call_target="tpu_custom_call" | custom-call | tf_op jit(solution)/shard_map/taps/pallas_call | solution.py:188
  2.3 20.4 %all_to_all.15.in_ref = bf16[16,72,128]{2,1,0:T(8,128)(2,1)S(1)} all-to-all(bf16[16,72,128]{2,1,0:T(8,128)(2,1)S(1)} %taps.1), channel_id=1, replica_groups=mesh['zh'=2,'y'=8,'x'=4,'zq'=3,'zr'=2,'c'=2] {'x','zr','c'}, dimensions={0} | all-to-all | bytes 589824 | tf_op jit(solution)/shard_map/all_to_all | solution.py:202
  22.6 0.2 sum.1
  22.9 33.6 %all_to_all.16.in_ref = bf16[48,32,128]{2,1,0:T(8,128)(2,1)S(1)} all-to-all(bf16[48,32,128]{2,1,0:T(8,128)(2,1)S(1)} %bitcast.2), channel_id=1, replica_groups=mesh['zh'=2,'y'=8,'x'=4,'zq'=3,'zr'=2,'c'=2] {'y','zq','zh'}, dimensions={0} | all-to-all | bytes 786432 | tf_op jit(solution)/shard_map/all_to_all | solution.py:213
  56.5 2.2 %correlate.1 = bf16[16,48,128]{2,1,0:T(8,128)(2,1)S(1)} custom-call(bf16[48,32,128]{2,1,0:T(8,128)(2,1)S(1)} %all_to_all.16.in_ref, f32[8,128]{1,0:T(8,128)S(1)} %get-tuple-element.8.tiles_ref), custom_call_target="tpu_custom_call" | custom-call | tf_op jit(solution)/shard_map/correlate/pallas_call | solution.py:214
  58.7 13.9 %all_to_all.17.in_ref = bf16[16,48,128]{2,1,0:T(8,128)(2,1)S(1)} all-to-all(bf16[16,48,128]{2,1,0:T(8,128)(2,1)S(1)} %correlate.1), channel_id=1, replica_groups=mesh['zh'=2,'y'=8,'x'=4,'zq'=3,'zr'=2,'c'=2] {'x','zr','c'}, dimensions={0} | all-to-all | bytes 393216 | tf_op jit(solution)/shard_map/all_to_all | solution.py:226
  72.6 0.8 %place.1 = f32[11,64,128]{2,1,0:T(8,128)} custom-call(bf16[16,48,128]{2,1,0:T(8,128)(2,1)S(1)} %all_to_all.17.in_ref), custom_call_target="tpu_custom_call" | custom-call | tf_op jit(solution)/shard_map/place/pallas_call | solution.py:227

commit v9 on v8

--- a/solution.py
+++ b/solution.py
@@ -15,7 +15,9 @@
 TAPS = 4
 FRAMES = 4 + TAPS - 1
 LANES = 128
-ZH, Y, X, ZQ, ZR, C = 2, 8, 4, 3, 2, 2
+ZH, YA, YB, X, ZQ, ZR, C = 2, 4, 2, 4, 3, 2, 2
+Y = YA * YB
+CT_AXES = ("zh", "ya", "yb")
 TILE_AXES = ("x", "zq", "zr", "c")
 OWN = 11
 SLOT = 12
@@ -26,8 +28,8 @@
 
 
 def dft_table():
-    x, zr, c, zh, y = np.meshgrid(*(np.arange(n) for n in (X, ZR, C, ZH, Y)), indexing="ij")
-    first = ((zh * Y + y) * 64 + ((x * ZR + zr) * C + c) * 4).reshape(-1)
+    x, zr, c, yb, zh, ya = np.meshgrid(*(np.arange(n) for n in (X, ZR, C, YB, ZH, YA)), indexing="ij")
+    first = ((zh * Y + ya * YB + yb) * 64 + ((x * ZR + zr) * C + c) * 4).reshape(-1)
     channels = first[:, None] + np.arange(4)[None, :]
     products = channels[:, :, None] * np.arange(QUARTER)[None, None, :] % NCHAN
     angles = products.astype(np.float32) * np.float32(2.0 * math.pi / NCHAN)
@@ -91,8 +93,7 @@
         table = table_ref[:, j * 2 * QUARTER : (j + 1) * 2 * QUARTER]
         high, low = split(jnp.concatenate(lives[j], axis=0))
         outs.append(dot(table, high, (1, 1)) + dot(table, low, (1, 1)))
-    for k, part in enumerate(swap_chunks(outs, 32)):
-        out_ref[:, k * 16 : (k + 1) * 16, :] = part.astype(BF).reshape(16, 16, LANES)
+    parts = [part.reshape(32, 8, LANES) for part in swap_chunks(outs, 32)]
 
     copies[2].wait()
     sub = lax.broadcasted_iota(jnp.int32, (8, LANES), 0)
@@ -102,35 +103,40 @@
     tiles = jnp.zeros((8, LANES), jnp.int32)
     for l in range(OWN):
         tiles = jnp.where(place == l, jnp.where(sub < 2, map_ref[0, l], map_ref[1, l]), tiles)
-    tiles = jnp.where((sub < 4) & (lane < 8 * SLOT), tiles, 0).astype(F32).astype(BF)
-    for d in range(16):
-        out_ref[d, 64:72, :] = tiles
-
-
-def sum_kernel(in_ref, out_ref, tiles_ref, f_ref):
+    tiles = jnp.where((sub < 4) & (lane < 8 * SLOT), tiles, 0).astype(F32)
+    parts.append(jnp.broadcast_to(tiles[None], (32, 8, LANES)))
+    out_ref[...] = jnp.concatenate(parts, axis=1).astype(BF)
+
+
+def sum_kernel(in_ref, out_ref, tiles_ref, g_ref, f_ref):
+    g_ref[...] = in_ref[...].astype(F32).reshape(g_ref.shape)
     for x in range(X):
-        for f in range(FRAMES):
-            total = None
-            for k in range(TAPS):
-                if 0 <= f - k < 4:
-                    part = in_ref[x * 4 + f - k, k * 16 : (k + 1) * 16, :].astype(F32)
-                    total = part if total is None else total + part
-            f_ref[pl.ds(x * 8 + f, ZH * Y, stride=32), :] = total
-        f_ref[pl.ds(x * 8 + FRAMES, ZH * Y, stride=32), :] = jnp.zeros((ZH * Y, LANES), F32)
+        for yb in range(YB):
+            for f in range(FRAMES):
+                total = None
+                for k in range(TAPS):
+                    if 0 <= f - k < 4:
+                        at = ((x * 4 + f - k) * YB + yb) * 40 + k * 8
+                        part = g_ref[at : at + 8, :]
+                        total = part if total is None else total + part
+                f_ref[pl.ds(f * 8 + x * YB + yb, ZH * YA, stride=56), :] = total
     for zh in range(ZH):
-        block = f_ref[zh * 256 : (zh + 1) * 256, :].reshape(Y, 32, LANES).astype(BF)
+        block = f_ref[zh * YA * 56 : (zh + 1) * YA * 56, :].reshape(YA, 56, LANES).astype(BF)
         for zq in range(ZQ):
             out_ref[:, zq * ZH + zh] = block
-    tiles_ref[...] = sum(in_ref[d, 64:72, :].astype(F32) for d in range(16))
+    tiles_ref[...] = sum(g_ref[d * YB * 40 + 32 : d * YB * 40 + 40, :] for d in range(16))
 
 
 def correlate_kernel(in_ref, tiles_ref, out_ref, f_ref, a_ref, c_ref, d_ref):
-    f_ref[...] = in_ref[...].astype(F32).reshape(f_ref.shape)
-    upper = lax.broadcasted_iota(jnp.int32, (8, LANES), 0) < 4
+    f_ref[: 24 * 56, :] = in_ref[...].astype(F32).reshape(24 * 56, LANES)
+    f_ref[24 * 56 :, :] = jnp.zeros((8, LANES), F32)
+    row = lax.broadcasted_iota(jnp.int32, (8, LANES), 0)
+    upper = row < 4
 
     def frames(zh, y):
-        at = [((y * ZQ + q % ZQ) * ZH + zh) * 32 + q // ZQ * 8 for q in range(X * ZQ)]
-        own = [f_ref[a : a + 8, :] for a in at]
+        ya, yb = divmod(y, YB)
+        at = [((ya * ZQ + q % ZQ) * ZH + zh) * 56 + q // ZQ * YB + yb for q in range(X * ZQ)]
+        own = [jnp.where(row < FRAMES, f_ref[pl.ds(a, 8, stride=8), :], 0.0) for a in at]
         turned = [pltpu.roll(v, 4, 0) for v in own]
         before = [jnp.zeros((8, LANES), F32)] + turned
         return jnp.concatenate(
@@ -187,7 +193,7 @@
     arrays = (tile_map.T, voltages, fir_taps, jnp.asarray(dft_table()))
     sent = pl.pallas_call(
         tap_kernel,
-        out_shape=jax.ShapeDtypeStruct((X * ZR * C, 72, LANES), BF),
+        out_shape=jax.ShapeDtypeStruct((X * ZR * C * YB, 40, LANES), BF),
         in_specs=[hbm] * 4,
         scratch_shapes=[
             pltpu.SMEM((2, OWN), jnp.int32),
@@ -199,23 +205,23 @@
         compiler_params=PARAMS,
         name="taps",
     )(*(pltpu.with_memory_space_constraint(a, pltpu.MemorySpace.HBM) for a in arrays))
-    came = lax.all_to_all(sent, ("x", "zr", "c"), 0, 0, tiled=True)
+    came = lax.all_to_all(sent, ("x", "zr", "c", "yb"), 0, 0, tiled=True)
     sent, tiles = pl.pallas_call(
         sum_kernel,
         out_shape=(
-            jax.ShapeDtypeStruct((Y, ZQ * ZH, 32, LANES), BF),
+            jax.ShapeDtypeStruct((YA, ZQ * ZH, 56, LANES), BF),
             jax.ShapeDtypeStruct((8, LANES), F32),
         ),
-        scratch_shapes=[pltpu.VMEM((ZH * Y * 32, LANES), F32)],
+        scratch_shapes=[pltpu.VMEM((32 * 40, LANES), F32), pltpu.VMEM((ZH * YA * 56, LANES), F32)],
         compiler_params=PARAMS,
         name="sum",
     )(came)
-    came = lax.all_to_all(sent.reshape(Y * ZQ * ZH, 32, LANES), ("y", "zq", "zh"), 0, 0, tiled=True)
+    came = lax.all_to_all(sent.reshape(YA * ZQ * ZH, 56, LANES), ("ya", "zq", "zh"), 0, 0, tiled=True)
     sent = pl.pallas_call(
         correlate_kernel,
         out_shape=jax.ShapeDtypeStruct((16, 4 * SLOT, LANES), BF),
         scratch_shapes=[
-            pltpu.VMEM((ZH * ZQ * Y * 32, LANES), F32),
+            pltpu.VMEM((24 * 56 + 8, LANES), F32),
             pltpu.VMEM((4, 2 * TIME, 256), BF),
             pltpu.VMEM((512, 256), F32),
             pltpu.VMEM((768, 512), BF),
@@ -234,7 +240,7 @@
 
 
 def solution(mesh):
-    fine = Mesh(mesh.devices.reshape(ZH, Y, X, ZQ, ZR, C), ("zh", "y") + TILE_AXES)
-    in_specs = (P(TILE_AXES, ("zh", "y"), None), P(), P(TILE_AXES, None))
-    out_specs = P(TILE_AXES, ("zh", "y"), None)
+    fine = Mesh(mesh.devices.reshape(ZH, YA, YB, X, ZQ, ZR, C), CT_AXES + TILE_AXES)
+    in_specs = (P(TILE_AXES, CT_AXES, None), P(), P(TILE_AXES, None))
+    out_specs = P(TILE_AXES, CT_AXES, None)
     return jax.shard_map(per_device, mesh=fine, in_specs=in_specs, out_specs=out_specs, check_vma=False)

time: 73.7 us -> 72.8 us (0.988)
  blocking collectives: 67.8 us -> 67 us
    all_to_all x2 -> x1, blocking collectives: 34.3 us -> 12.1 us  [per_device(): came = lax.all_to_all(sent, ('x', 'zr', 'c'), 0, 0, tiled=True)]
    all_to_all x1 -> x2, blocking collectives: 33.6 us -> 54.9 us  [the longest x1 32.5 us: per_device(): lax.all_to_all(sent.reshape(YA * ZQ * ZH, 56, LANES), ('ya', 'zq', 'zh'),...]
where the time goes in v9:
time: 72.8 us; the launch traced here: 72.6 us
  blocking collectives  67 us (92%)
  Pallas kernels  5.51 us (8%)
    all_to_all x1, blocking collectives, per_device(): lax.all_to_all(sent.reshape(YA * ZQ * ZH, 56, LANES), ('ya', 'zq', 'zh'),...  32.5 us
    all_to_all x1, blocking collectives, per_device(): came = lax.all_to_all(sent, ('x', 'zr', 'c', 'yb'), 0, 0, tiled=True)  22.4 us
    all_to_all x1, blocking collectives, per_device(): came = lax.all_to_all(sent, ('x', 'zr', 'c'), 0, 0, tiled=True)  12.1 us
    pallas_call x1, Pallas kernels, per_device(): pl.pallas_call(correlate_kernel, out_shape=jax.ShapeDtypeStruct((16, 4 *...  2.37 us
    pallas_call x1, Pallas kernels, per_device(): pl.pallas_call(tap_kernel, out_shape=jax.ShapeDtypeStruct((X * ZR * C * Y...  2.26 us

profile of v9, /device:TPU:1, one launch (start us, length us, event | category | flops | bytes accessed | tf_op | source)
XLA Modules:
  0.0 72.6 jit_solution(18015660370902007370)
XLA Ops:
  0.0 2.3 %taps.1 = bf16[32,40,128]{2,1,0:T(8,128)(2,1)S(1)} custom-call(s32[2,11]{1,0:T(2,128)} %bitcast.3, s32[1,16,2048]{2,1,0:T(8,128)} %volts_hbm.1, f32[4,1024]{1,0:T(4,128)} %fir_hbm.1, bf16[256,2048]{1,0:T(8,128)(2,1)} %constant.2.clone.table_hbm), custom_call_target="tpu_custom_call" | custom-call | tf_op jit(solution)/shard_map/taps/pallas_call | solution.py:194
  2.3 22.4 %all_to_all.15.in_ref = bf16[32,40,128]{2,1,0:T(8,128)(2,1)S(1)} all-to-all(bf16[32,40,128]{2,1,0:T(8,128)(2,1)S(1)} %taps.1), channel_id=1, replica_groups=mesh['zh'=2,'ya'=4,'yb'=2,'x'=4,'zq'=3,'zr'=2,'c'=2] {'x','zr','c','yb'}, dimensions={0} | all-to-all | bytes 655360 | tf_op jit(solution)/shard_map/all_to_all | solution.py:208
  24.7 0.1 sum.1
  24.8 32.5 %all_to_all.16.in_ref = bf16[24,56,128]{2,1,0:T(8,128)(2,1)S(1)} all-to-all(bf16[24,56,128]{2,1,0:T(8,128)(2,1)S(1)} %bitcast.2), channel_id=1, replica_groups=mesh['zh'=2,'ya'=4,'yb'=2,'x'=4,'zq'=3,'zr'=2,'c'=2] {'ya','zq','zh'}, dimensions={0} | all-to-all | bytes 688128 | tf_op jit(solution)/shard_map/all_to_all | solution.py:219
  57.3 2.4 %correlate.1 = bf16[16,48,128]{2,1,0:T(8,128)(2,1)S(1)} custom-call(bf16[24,56,128]{2,1,0:T(8,128)(2,1)S(1)} %all_to_all.16.in_ref, f32[8,128]{1,0:T(8,128)S(1)} %get-tuple-element.8.tiles_ref), custom_call_target="tpu_custom_call" | custom-call | tf_op jit(solution)/shard_map/correlate/pallas_call | solution.py:220
  59.7 12.1 %all_to_all.17.in_ref = bf16[16,48,128]{2,1,0:T(8,128)(2,1)S(1)} all-to-all(bf16[16,48,128]{2,1,0:T(8,128)(2,1)S(1)} %correlate.1), channel_id=1, replica_groups=mesh['zh'=2,'ya'=4,'yb'=2,'x'=4,'zq'=3,'zr'=2,'c'=2] {'x','zr','c'}, dimensions={0} | all-to-all | bytes 393216 | tf_op jit(solution)/shard_map/all_to_all | solution.py:232
  71.8 0.8 %place.1 = f32[11,64,128]{2,1,0:T(8,128)} custom-call(bf16[16,48,128]{2,1,0:T(8,128)(2,1)S(1)} %all_to_all.17.in_ref), custom_call_target="tpu_custom_call" | custom-call | tf_op jit(solution)/shard_map/place/pallas_call | solution.py:233

commit v10 on v9

--- a/solution.py
+++ b/solution.py
@@ -35,7 +35,7 @@
     angles = products.astype(np.float32) * np.float32(2.0 * math.pi / NCHAN)
     scale = np.float32(1.0 / math.sqrt(NCHAN))
     both = np.stack([np.cos(angles) * scale, np.sin(angles) * scale], axis=2)
-    return both.reshape(256, 8 * QUARTER).astype(ml_dtypes.bfloat16)
+    return both.transpose(1, 0, 2, 3).reshape(4, 256, 2 * QUARTER).astype(ml_dtypes.bfloat16)
 
 
 def swap_chunks(rows, width):
@@ -63,7 +63,8 @@
 
 
 def tap_kernel(map_hbm, volts_hbm, fir_hbm, table_hbm, out_ref, map_ref, volts_ref, fir_ref, table_ref, sems):
-    pairs = ((volts_hbm.at[0], volts_ref), (fir_hbm, fir_ref), (map_hbm, map_ref), (table_hbm, table_ref))
+    pairs = [(volts_hbm.at[0], volts_ref), (fir_hbm, fir_ref), (map_hbm, map_ref)]
+    pairs += [(table_hbm.at[j], table_ref.at[j]) for j in range(4)]
     copies = [pltpu.make_async_copy(src, dst, sems.at[i]) for i, (src, dst) in enumerate(pairs)]
     for copy in copies:
         copy.start()
@@ -87,10 +88,10 @@
         )
         for j, (r, m) in enumerate(sums):
             lives[j] += [jnp.concatenate([r, m], axis=1), jnp.concatenate([m, -r], axis=1)]
-    copies[3].wait()
     outs = []
     for j in range(4):
-        table = table_ref[:, j * 2 * QUARTER : (j + 1) * 2 * QUARTER]
+        copies[3 + j].wait()
+        table = table_ref[j]
         high, low = split(jnp.concatenate(lives[j], axis=0))
         outs.append(dot(table, high, (1, 1)) + dot(table, low, (1, 1)))
     parts = [part.reshape(32, 8, LANES) for part in swap_chunks(outs, 32)]
@@ -129,7 +130,7 @@
 
 def correlate_kernel(in_ref, tiles_ref, out_ref, f_ref, a_ref, c_ref, d_ref):
     f_ref[: 24 * 56, :] = in_ref[...].astype(F32).reshape(24 * 56, LANES)
-    f_ref[24 * 56 :, :] = jnp.zeros((8, LANES), F32)
+    f_ref[24 * 56 :, :] = jnp.zeros((64, LANES), F32)
     row = lax.broadcasted_iota(jnp.int32, (8, LANES), 0)
     upper = row < 4
 
@@ -180,7 +181,7 @@
 
 
 def place_kernel(in_ref, out_ref, f_ref):
-    f_ref[...] = in_ref[...].astype(F32).reshape(f_ref.shape)
+    f_ref[: 16 * 48, :] = in_ref[...].astype(F32).reshape(16 * 48, LANES)
     for l in range(OWN):
         out_ref[l] = f_ref[pl.ds(l, 64, stride=SLOT), :]
 
@@ -199,8 +200,8 @@
             pltpu.SMEM((2, OWN), jnp.int32),
             pltpu.VMEM((16, 2 * NCHAN), jnp.int32),
             pltpu.VMEM((TAPS, NCHAN), F32),
-            pltpu.VMEM((256, 8 * QUARTER), BF),
-            pltpu.SemaphoreType.DMA((4,)),
+            pltpu.VMEM((4, 256, 2 * QUARTER), BF),
+            pltpu.SemaphoreType.DMA((7,)),
         ],
         compiler_params=PARAMS,
         name="taps",
@@ -212,7 +213,7 @@
             jax.ShapeDtypeStruct((YA, ZQ * ZH, 56, LANES), BF),
             jax.ShapeDtypeStruct((8, LANES), F32),
         ),
-        scratch_shapes=[pltpu.VMEM((32 * 40, LANES), F32), pltpu.VMEM((ZH * YA * 56, LANES), F32)],
+        scratch_shapes=[pltpu.VMEM((32 * 40, LANES), F32), pltpu.VMEM((ZH * YA * 56 + 56, LANES), F32)],
         compiler_params=PARAMS,
         name="sum",
     )(came)
@@ -221,7 +222,7 @@
         correlate_kernel,
         out_shape=jax.ShapeDtypeStruct((16, 4 * SLOT, LANES), BF),
         scratch_shapes=[
-            pltpu.VMEM((24 * 56 + 8, LANES), F32),
+            pltpu.VMEM((24 * 56 + 64, LANES), F32),
             pltpu.VMEM((4, 2 * TIME, 256), BF),
             pltpu.VMEM((512, 256), F32),
             pltpu.VMEM((768, 512), BF),
@@ -233,7 +234,7 @@
     return pl.pallas_call(
         place_kernel,
         out_shape=jax.ShapeDtypeStruct((OWN, 64, LANES), F32),
-        scratch_shapes=[pltpu.VMEM((16 * 4 * SLOT, LANES), F32)],
+        scratch_shapes=[pltpu.VMEM((16 * 4 * SLOT + 16, LANES), F32)],
         compiler_params=PARAMS,
         name="place",
     )(came)

time: 72.8 us -> 73.5 us (level)
  no operation moved by 1% of the time
where the time goes in v10:
time: 73.5 us; the launch traced here: 73.3 us
  blocking collectives  67 us (91%)
  Pallas kernels  6.21 us (8%)
    all_to_all x1, blocking collectives, per_device(): lax.all_to_all(sent.reshape(YA * ZQ * ZH, 56, LANES), ('ya', 'zq', 'zh'),...  32.6 us
    all_to_all x1, blocking collectives, per_device(): came = lax.all_to_all(sent, ('x', 'zr', 'c', 'yb'), 0, 0, tiled=True)  22.4 us
    all_to_all x1, blocking collectives, per_device(): came = lax.all_to_all(sent, ('x', 'zr', 'c'), 0, 0, tiled=True)  12.1 us
    pallas_call x1, Pallas kernels, per_device(): pl.pallas_call(tap_kernel, out_shape=jax.ShapeDtypeStruct((X * ZR * C * Y...  2.97 us
    pallas_call x1, Pallas kernels, per_device(): pl.pallas_call(correlate_kernel, out_shape=jax.ShapeDtypeStruct((16, 4 *...  2.37 us

profile of v10, /device:TPU:1, one launch (start us, length us, event | category | flops | bytes accessed | tf_op | source)
XLA Modules:
  0.0 73.3 jit_solution(16377794742706696654)
XLA Ops:
  0.0 3.0 %taps.1 = bf16[32,40,128]{2,1,0:T(8,128)(2,1)S(1)} custom-call(s32[2,11]{1,0:T(2,128)} %bitcast.3, s32[1,16,2048]{2,1,0:T(8,128)} %volts_hbm.1, f32[4,1024]{1,0:T(4,128)} %fir_hbm.1, bf16[4,256,512]{2,1,0:T(8,128)(2,1)} %constant.2.clone.table_hbm), custom_call_target="tpu_custom_call" | custom-call | tf_op jit(solution)/shard_map/taps/pallas_call | solution.py:195
  3.0 22.4 %all_to_all.15.in_ref = bf16[32,40,128]{2,1,0:T(8,128)(2,1)S(1)} all-to-all(bf16[32,40,128]{2,1,0:T(8,128)(2,1)S(1)} %taps.1), channel_id=1, replica_groups=mesh['zh'=2,'ya'=4,'yb'=2,'x'=4,'zq'=3,'zr'=2,'c'=2] {'x','zr','c','yb'}, dimensions={0} | all-to-all | bytes 655360 | tf_op jit(solution)/shard_map/all_to_all | solution.py:209
  25.4 0.1 sum.1
  25.5 32.6 %all_to_all.16.in_ref = bf16[24,56,128]{2,1,0:T(8,128)(2,1)S(1)} all-to-all(bf16[24,56,128]{2,1,0:T(8,128)(2,1)S(1)} %bitcast.2), channel_id=1, replica_groups=mesh['zh'=2,'ya'=4,'yb'=2,'x'=4,'zq'=3,'zr'=2,'c'=2] {'ya','zq','zh'}, dimensions={0} | all-to-all | bytes 688128 | tf_op jit(solution)/shard_map/all_to_all | solution.py:220
  58.0 2.4 %correlate.1 = bf16[16,48,128]{2,1,0:T(8,128)(2,1)S(1)} custom-call(bf16[24,56,128]{2,1,0:T(8,128)(2,1)S(1)} %all_to_all.16.in_ref, f32[8,128]{1,0:T(8,128)S(1)} %get-tuple-element.8.tiles_ref), custom_call_target="tpu_custom_call" | custom-call | tf_op jit(solution)/shard_map/correlate/pallas_call | solution.py:221
  60.4 12.1 %all_to_all.17.in_ref = bf16[16,48,128]{2,1,0:T(8,128)(2,1)S(1)} all-to-all(bf16[16,48,128]{2,1,0:T(8,128)(2,1)S(1)} %correlate.1), channel_id=1, replica_groups=mesh['zh'=2,'ya'=4,'yb'=2,'x'=4,'zq'=3,'zr'=2,'c'=2] {'x','zr','c'}, dimensions={0} | all-to-all | bytes 393216 | tf_op jit(solution)/shard_map/all_to_all | solution.py:233
  72.5 0.8 %place.1 = f32[11,64,128]{2,1,0:T(8,128)} custom-call(bf16[16,48,128]{2,1,0:T(8,128)(2,1)S(1)} %all_to_all.17.in_ref), custom_call_target="tpu_custom_call" | custom-call | tf_op jit(solution)/shard_map/place/pallas_call | solution.py:234

commit v11 on v10

--- a/solution.py
+++ b/solution.py
@@ -63,8 +63,7 @@
 
 
 def tap_kernel(map_hbm, volts_hbm, fir_hbm, table_hbm, out_ref, map_ref, volts_ref, fir_ref, table_ref, sems):
-    pairs = [(volts_hbm.at[0], volts_ref), (fir_hbm, fir_ref), (map_hbm, map_ref)]
-    pairs += [(table_hbm.at[j], table_ref.at[j]) for j in range(4)]
+    pairs = ((volts_hbm.at[0], volts_ref), (fir_hbm, fir_ref), (map_hbm, map_ref), (table_hbm, table_ref))
     copies = [pltpu.make_async_copy(src, dst, sems.at[i]) for i, (src, dst) in enumerate(pairs)]
     for copy in copies:
         copy.start()
@@ -88,9 +87,9 @@
         )
         for j, (r, m) in enumerate(sums):
             lives[j] += [jnp.concatenate([r, m], axis=1), jnp.concatenate([m, -r], axis=1)]
+    copies[3].wait()
     outs = []
     for j in range(4):
-        copies[3 + j].wait()
         table = table_ref[j]
         high, low = split(jnp.concatenate(lives[j], axis=0))
         outs.append(dot(table, high, (1, 1)) + dot(table, low, (1, 1)))
@@ -201,7 +200,7 @@
             pltpu.VMEM((16, 2 * NCHAN), jnp.int32),
             pltpu.VMEM((TAPS, NCHAN), F32),
             pltpu.VMEM((4, 256, 2 * QUARTER), BF),
-            pltpu.SemaphoreType.DMA((7,)),
+            pltpu.SemaphoreType.DMA((4,)),
         ],
         compiler_params=PARAMS,
         name="taps",

time: 73.5 us -> 72.8 us (level)
  no operation moved by 1% of the time
where the time goes in v11:
time: 72.8 us; the launch traced here: 72.6 us
  blocking collectives  67 us (92%)
  Pallas kernels  5.5 us (8%)
    all_to_all x1, blocking collectives, per_device(): lax.all_to_all(sent.reshape(YA * ZQ * ZH, 56, LANES), ('ya', 'zq', 'zh'),...  32.6 us
    all_to_all x1, blocking collectives, per_device(): came = lax.all_to_all(sent, ('x', 'zr', 'c', 'yb'), 0, 0, tiled=True)  22.4 us
    all_to_all x1, blocking collectives, per_device(): came = lax.all_to_all(sent, ('x', 'zr', 'c'), 0, 0, tiled=True)  12.1 us
    pallas_call x1, Pallas kernels, per_device(): pl.pallas_call(correlate_kernel, out_shape=jax.ShapeDtypeStruct((16, 4 *...  2.38 us
    pallas_call x1, Pallas kernels, per_device(): pl.pallas_call(tap_kernel, out_shape=jax.ShapeDtypeStruct((X * ZR * C * Y...  2.25 us

profile of v11, /device:TPU:1, one launch (start us, length us, event | category | flops | bytes accessed | tf_op | source)
XLA Modules:
  0.0 72.6 jit_solution(145582938401967934)
XLA Ops:
  0.0 2.2 %taps.1 = bf16[32,40,128]{2,1,0:T(8,128)(2,1)S(1)} custom-call(s32[2,11]{1,0:T(2,128)} %bitcast.3, s32[1,16,2048]{2,1,0:T(8,128)} %volts_hbm.1, f32[4,1024]{1,0:T(4,128)} %fir_hbm.1, bf16[4,256,512]{2,1,0:T(8,128)(2,1)} %constant.2.clone.table_hbm), custom_call_target="tpu_custom_call" | custom-call | tf_op jit(solution)/shard_map/taps/pallas_call | solution.py:194
  2.3 22.4 %all_to_all.15.in_ref = bf16[32,40,128]{2,1,0:T(8,128)(2,1)S(1)} all-to-all(bf16[32,40,128]{2,1,0:T(8,128)(2,1)S(1)} %taps.1), channel_id=1, replica_groups=mesh['zh'=2,'ya'=4,'yb'=2,'x'=4,'zq'=3,'zr'=2,'c'=2] {'x','zr','c','yb'}, dimensions={0} | all-to-all | bytes 655360 | tf_op jit(solution)/shard_map/all_to_all | solution.py:208
  24.7 0.1 sum.1
  24.7 32.6 %all_to_all.16.in_ref = bf16[24,56,128]{2,1,0:T(8,128)(2,1)S(1)} all-to-all(bf16[24,56,128]{2,1,0:T(8,128)(2,1)S(1)} %bitcast.2), channel_id=1, replica_groups=mesh['zh'=2,'ya'=4,'yb'=2,'x'=4,'zq'=3,'zr'=2,'c'=2] {'ya','zq','zh'}, dimensions={0} | all-to-all | bytes 688128 | tf_op jit(solution)/shard_map/all_to_all | solution.py:219
  57.3 2.4 %correlate.1 = bf16[16,48,128]{2,1,0:T(8,128)(2,1)S(1)} custom-call(bf16[24,56,128]{2,1,0:T(8,128)(2,1)S(1)} %all_to_all.16.in_ref, f32[8,128]{1,0:T(8,128)S(1)} %get-tuple-element.8.tiles_ref), custom_call_target="tpu_custom_call" | custom-call | tf_op jit(solution)/shard_map/correlate/pallas_call | solution.py:220
  59.7 12.1 %all_to_all.17.in_ref = bf16[16,48,128]{2,1,0:T(8,128)(2,1)S(1)} all-to-all(bf16[16,48,128]{2,1,0:T(8,128)(2,1)S(1)} %correlate.1), channel_id=1, replica_groups=mesh['zh'=2,'ya'=4,'yb'=2,'x'=4,'zq'=3,'zr'=2,'c'=2] {'x','zr','c'}, dimensions={0} | all-to-all | bytes 393216 | tf_op jit(solution)/shard_map/all_to_all | solution.py:232
  71.8 0.8 %place.1 = f32[11,64,128]{2,1,0:T(8,128)} custom-call(bf16[16,48,128]{2,1,0:T(8,128)(2,1)S(1)} %all_to_all.17.in_ref), custom_call_target="tpu_custom_call" | custom-call | tf_op jit(solution)/shard_map/place/pallas_call | solution.py:233
